TPU v7x, 32 devices: a whole 2x2x4 slice. The times are simulated.
32 devices in a mesh: rep: 4 (over y, x), fsdp: 8 (over z, core).
Axes of the slice: x: 2, y: 2, z: 4, core: 2. Of those that a mesh axis runs over, the one named last changes fastest.
Arguments:
- tokens: bfloat16 [73728, 768], P(('rep', 'fsdp')), may hold values from -6 to 6
- cotangent: bfloat16 [73728, 768], P(('rep', 'fsdp')), may hold values from -6 to 6
- crop_heights: int32 [128], P(('rep', 'fsdp')), may hold values from 12 to 24, as said below
- rope_positions: int32 [128, 2, 576], P(('rep', 'fsdp')), may hold values from 0 to 31, as said below
- gain_attn: bfloat16 [768], P('fsdp'), may hold values from 0.5 to 1.5
- w_query: bfloat16 [768, 768], P('fsdp'), may hold values from -0.21875 to 0.21875
- w_key: bfloat16 [768, 768], P('fsdp'), may hold values from -0.21875 to 0.21875
- w_value: bfloat16 [768, 768], P('fsdp'), may hold values from -0.21875 to 0.21875
- w_out: bfloat16 [768, 768], P('fsdp'), may hold values from -0.875 to 0.875
- gain_mlp: bfloat16 [768], P('fsdp'), may hold values from 0.5 to 1.5
- w_gate: bfloat16 [768, 2048], P('fsdp'), may hold values from -0.21875 to 0.21875
- w_up: bfloat16 [768, 2048], P('fsdp'), may hold values from -0.21875 to 0.21875
- w_down: bfloat16 [2048, 768], P('fsdp'), may hold values from -0.125 to 0.125
Outputs:
- out_tokens: bfloat16 [73728, 768], P(('rep', 'fsdp'))
- grad_tokens: float32 [73728, 768], P(('rep', 'fsdp'))
- grad_gain_attn: float32 [768], P('fsdp')
- grad_query: float32 [768, 768], P('fsdp')
- grad_key: float32 [768, 768], P('fsdp')
- grad_value: float32 [768, 768], P('fsdp')
- grad_out: float32 [768, 768], P('fsdp')
- grad_gain_mlp: float32 [768], P('fsdp')
- grad_gate: float32 [768, 2048], P('fsdp')
- grad_up: float32 [768, 2048], P('fsdp')
- grad_down: float32 [2048, 768], P('fsdp')
Inputs may be any that keep to these rules, and one draw needn't show every extreme that they name: Crop c holds 24 * crop_heights[c] valid tokens in the first slots of its 576; the rest are padding. `rope_positions`: the valid slots of a crop lie on consecutive grid rows starting at some row, 24 consecutive columns each, in row-major order; padding slots carry positions too.
All inputs are finite; a program needn't handle non-finite values.
Results may differ from a plain program's by a relative error of at most 0.015.
Values may be sent and summed in bfloat16 or wider, within the bound.
No kernel may reach another device: no remote copies, remote signals or barrier semaphores. Data moves between devices by JAX's collectives and lax.ppermute only.
A program may use at most 256 MiB of HBM per device.

v0:
```python
import jax
import jax.numpy as jnp
from jax import lax
from jax.sharding import PartitionSpec as P

HEAD_DIM = 64
COLS = 24


EPSILON = 1e-05
NEGATIVE = -1e30
HEAD_BLOCK = 4


def across(left, right):
    return lax.dot_general(
        left, right, (((0,), (0,)), ((), ())), preferred_element_type=jnp.float32
    )


def through(left, right):
    return lax.dot_general(
        left, right, (((1,), (1,)), ((), ())), preferred_element_type=jnp.float32
    )


def angle_tables(positions):
    frequency = 1.0 / 10000.0 ** (jnp.arange(HEAD_DIM // 4, dtype=jnp.float32) * 4.0 / HEAD_DIM)
    row_angle = positions[:, 0, :, None].astype(jnp.float32) * frequency
    col_angle = positions[:, 1, :, None].astype(jnp.float32) * frequency
    angles = jnp.concatenate([row_angle, col_angle], axis=-1)
    return (jnp.cos(angles)[:, :, None, :], jnp.sin(angles)[:, :, None, :])


def rotate(field, cosine, sine_table):
    half_dim = field.shape[-1] // 2
    first_half = field[..., :half_dim]
    second_half = field[..., half_dim:]
    return jnp.concatenate(
        [
            first_half * cosine - second_half * sine_table,
            first_half * sine_table + second_half * cosine,
        ],
        axis=-1,
    )


def inverse_rms(field):
    return lax.rsqrt(jnp.mean(field * field, axis=-1, keepdims=True) + EPSILON)


def norm_back(grad_normed, field, inverse, gain):
    scaled = grad_normed * gain
    grad_field = inverse * scaled - field * inverse**3 * jnp.mean(
        scaled * field, axis=-1, keepdims=True
    )
    return (grad_field, jnp.sum(grad_normed * field * inverse, axis=0))


def to_blocks(field):
    crop_count, slot_len, head_count, head_dim = field.shape
    return field.transpose(0, 2, 1, 3).reshape(
        crop_count * head_count // HEAD_BLOCK, HEAD_BLOCK, slot_len, head_dim
    )


def from_blocks(field, crop_count):
    block_count, block_heads, slot_len, head_dim = field.shape
    head_count = block_count * block_heads // crop_count
    return field.reshape(crop_count, head_count, slot_len, head_dim).transpose(0, 2, 1, 3)


def body(
    tokens,
    cotangent,
    crop_heights,
    rope_positions,
    gain_attn,
    w_query,
    w_key,
    w_value,
    w_out,
    gain_mlp,
    w_gate,
    w_up,
    w_down,
):
    crop_count = crop_heights.shape[0]
    row_count, model_width = tokens.shape
    slot_len = row_count // crop_count
    head_count = model_width // HEAD_DIM
    score_scale = HEAD_DIM ** (-0.5)
    causal = jnp.arange(slot_len)[:, None] >= jnp.arange(slot_len)[None, :]
    valid_rows = (
        (jnp.arange(slot_len)[None, :] < (crop_heights * COLS)[:, None])
        .astype(jnp.float32)
        .reshape(row_count, 1)
    )
    cosine, sine_table = angle_tables(rope_positions)
    attn_set = (
        lax.all_gather(gain_attn, "fsdp", axis=0, tiled=True),
        lax.all_gather(w_query, "fsdp", axis=0, tiled=True),
        lax.all_gather(w_key, "fsdp", axis=0, tiled=True),
        lax.all_gather(w_value, "fsdp", axis=0, tiled=True),
        lax.all_gather(w_out, "fsdp", axis=0, tiled=True),
    )
    inputs = tokens.astype(jnp.float32)
    inverse_one = inverse_rms(inputs)
    normed = (inputs * inverse_one * attn_set[0].astype(jnp.float32)).astype(jnp.bfloat16)

    def per_head(weight):
        return jnp.dot(normed, weight, preferred_element_type=jnp.float32).reshape(
            crop_count, slot_len, head_count, HEAD_DIM
        )

    queries = to_blocks(rotate(per_head(attn_set[1]), cosine, sine_table).astype(jnp.bfloat16))
    keys_rot = to_blocks(rotate(per_head(attn_set[2]), cosine, sine_table).astype(jnp.bfloat16))
    values_in = to_blocks(per_head(attn_set[3]).astype(jnp.bfloat16))

    def block_scores(query_block, key_block):
        scores = (
            jnp.einsum("hqd,hkd->hqk", query_block, key_block, preferred_element_type=jnp.float32)
            * score_scale
        )
        return jnp.where(causal, scores, NEGATIVE)

    def attend(member):
        scores = block_scores(member[0], member[1])
        maximum = jnp.max(scores, axis=-1, keepdims=True)
        exponent = jnp.exp(scores - maximum)
        row_total = jnp.sum(exponent, axis=-1, keepdims=True)
        probs_low = (exponent / row_total).astype(jnp.bfloat16)
        mixed = jnp.einsum("hqk,hkd->hqd", probs_low, member[2], preferred_element_type=jnp.float32)
        return (mixed.astype(jnp.bfloat16), maximum[..., 0] + jnp.log(row_total[..., 0]))

    attended_blocks, log_total = lax.map(attend, (queries, keys_rot, values_in))
    attended = from_blocks(attended_blocks, crop_count).reshape(row_count, model_width)
    middle = inputs + valid_rows * jnp.dot(
        attended, attn_set[4], preferred_element_type=jnp.float32
    )
    mlp_set = (
        lax.all_gather(gain_mlp, "fsdp", axis=0, tiled=True),
        lax.all_gather(w_gate, "fsdp", axis=0, tiled=True),
        lax.all_gather(w_up, "fsdp", axis=0, tiled=True),
        lax.all_gather(w_down, "fsdp", axis=0, tiled=True),
    )
    inverse_two = inverse_rms(middle)
    normed_mlp = (middle * inverse_two * mlp_set[0].astype(jnp.float32)).astype(jnp.bfloat16)
    gate_val = jnp.dot(normed_mlp, mlp_set[1], preferred_element_type=jnp.float32)
    up_val = jnp.dot(normed_mlp, mlp_set[2], preferred_element_type=jnp.float32)
    sigmoid_gate = jax.nn.sigmoid(gate_val)
    hidden = (gate_val * sigmoid_gate * up_val).astype(jnp.bfloat16)
    out_tokens = (
        middle + valid_rows * jnp.dot(hidden, mlp_set[3], preferred_element_type=jnp.float32)
    ).astype(jnp.bfloat16)
    mlp_back = (
        lax.all_gather(gain_mlp, "fsdp", axis=0, tiled=True),
        lax.all_gather(w_gate, "fsdp", axis=0, tiled=True),
        lax.all_gather(w_up, "fsdp", axis=0, tiled=True),
        lax.all_gather(w_down, "fsdp", axis=0, tiled=True),
    )
    mlp_left, hidden_left = (normed_mlp, hidden)
    grad_y = cotangent.astype(jnp.float32)
    grad_branch = (grad_y * valid_rows).astype(jnp.bfloat16)
    grad_down = across(hidden_left, grad_branch)
    grad_hidden = through(grad_branch, mlp_back[3])
    grad_gate_val = (
        grad_hidden * up_val * sigmoid_gate * (1.0 + gate_val * (1.0 - sigmoid_gate))
    ).astype(jnp.bfloat16)
    grad_up_val = (grad_hidden * gate_val * sigmoid_gate).astype(jnp.bfloat16)
    grad_gate = across(mlp_left, grad_gate_val)
    grad_up = across(mlp_left, grad_up_val)
    grad_normed_mlp = through(grad_gate_val, mlp_back[1]) + through(grad_up_val, mlp_back[2])
    grad_mid_part, grad_gain_mlp = norm_back(
        grad_normed_mlp, middle, inverse_two, mlp_back[0].astype(jnp.float32)
    )
    grad_middle = grad_y + grad_mid_part
    mlp_local = (
        lax.psum_scatter(grad_gain_mlp, "fsdp", scatter_dimension=0, tiled=True),
        lax.psum_scatter(grad_gate, "fsdp", scatter_dimension=0, tiled=True),
        lax.psum_scatter(grad_up, "fsdp", scatter_dimension=0, tiled=True),
        lax.psum_scatter(grad_down, "fsdp", scatter_dimension=0, tiled=True),
    )
    mlp_grads = (
        lax.psum(mlp_local[0].astype(jnp.bfloat16), "rep").astype(jnp.float32),
        lax.psum(mlp_local[1].astype(jnp.bfloat16), "rep").astype(jnp.float32),
        lax.psum(mlp_local[2].astype(jnp.bfloat16), "rep").astype(jnp.float32),
        lax.psum(mlp_local[3].astype(jnp.bfloat16), "rep").astype(jnp.float32),
    )
    attn_back = (
        lax.all_gather(gain_attn, "fsdp", axis=0, tiled=True),
        lax.all_gather(w_query, "fsdp", axis=0, tiled=True),
        lax.all_gather(w_key, "fsdp", axis=0, tiled=True),
        lax.all_gather(w_value, "fsdp", axis=0, tiled=True),
        lax.all_gather(w_out, "fsdp", axis=0, tiled=True),
    )
    normed_left, attended_left = (normed, attended)
    grad_attn_out = (grad_middle * valid_rows).astype(jnp.bfloat16)
    grad_wout = across(attended_left, grad_attn_out)
    grad_attended = through(grad_attn_out, attn_back[4]).astype(jnp.bfloat16)

    def attend_back(member):
        query_block, key_block, value_block, grad_block, log_block = member
        attn_probs = jnp.exp(block_scores(query_block, key_block) - log_block[..., None])
        grad_probs = jnp.einsum(
            "hqd,hkd->hqk", grad_block, value_block, preferred_element_type=jnp.float32
        )
        inner_sum = jnp.sum(attn_probs * grad_probs, axis=-1, keepdims=True)
        grad_scores = (attn_probs * (grad_probs - inner_sum)).astype(jnp.bfloat16)
        grad_query_block = (
            jnp.einsum("hqk,hkd->hqd", grad_scores, key_block, preferred_element_type=jnp.float32)
            * score_scale
        )
        grad_key_block = (
            jnp.einsum("hqk,hqd->hkd", grad_scores, query_block, preferred_element_type=jnp.float32)
            * score_scale
        )
        grad_value_block = jnp.einsum(
            "hqk,hqd->hkd",
            attn_probs.astype(jnp.bfloat16),
            grad_block,
            preferred_element_type=jnp.float32,
        )
        return (grad_query_block, grad_key_block, grad_value_block.astype(jnp.bfloat16))

    grad_att_blocks = to_blocks(grad_attended.reshape(crop_count, slot_len, head_count, HEAD_DIM))
    grad_q_blocks, grad_k_blocks, grad_v_blocks = lax.map(
        attend_back, (queries, keys_rot, values_in, grad_att_blocks, log_total)
    )
    grad_queries = (
        rotate(from_blocks(grad_q_blocks, crop_count), cosine, -sine_table)
        .reshape(row_count, model_width)
        .astype(jnp.bfloat16)
    )
    grad_keys = (
        rotate(from_blocks(grad_k_blocks, crop_count), cosine, -sine_table)
        .reshape(row_count, model_width)
        .astype(jnp.bfloat16)
    )
    grad_values = from_blocks(grad_v_blocks, crop_count).reshape(row_count, model_width)
    grad_wquery = across(normed_left, grad_queries)
    grad_wkey = across(normed_left, grad_keys)
    grad_wvalue = across(normed_left, grad_values)
    grad_normed = (
        through(grad_queries, attn_back[1])
        + through(grad_keys, attn_back[2])
        + through(grad_values, attn_back[3])
    )
    grad_in_part, grad_gain_attn = norm_back(
        grad_normed, inputs, inverse_one, attn_back[0].astype(jnp.float32)
    )
    grad_tokens = grad_middle + grad_in_part
    attn_local = (
        lax.psum_scatter(grad_gain_attn, "fsdp", scatter_dimension=0, tiled=True),
        lax.psum_scatter(grad_wquery, "fsdp", scatter_dimension=0, tiled=True),
        lax.psum_scatter(grad_wkey, "fsdp", scatter_dimension=0, tiled=True),
        lax.psum_scatter(grad_wvalue, "fsdp", scatter_dimension=0, tiled=True),
        lax.psum_scatter(grad_wout, "fsdp", scatter_dimension=0, tiled=True),
    )
    attn_grads = (
        lax.psum(attn_local[0].astype(jnp.bfloat16), "rep").astype(jnp.float32),
        lax.psum(attn_local[1].astype(jnp.bfloat16), "rep").astype(jnp.float32),
        lax.psum(attn_local[2].astype(jnp.bfloat16), "rep").astype(jnp.float32),
        lax.psum(attn_local[3].astype(jnp.bfloat16), "rep").astype(jnp.float32),
        lax.psum(attn_local[4].astype(jnp.bfloat16), "rep").astype(jnp.float32),
    )
    return (
        out_tokens,
        grad_tokens,
        attn_grads[0],
        attn_grads[1],
        attn_grads[2],
        attn_grads[3],
        attn_grads[4],
        mlp_grads[0],
        mlp_grads[1],
        mlp_grads[2],
        mlp_grads[3],
    )


def solution(mesh):
    in_specs = (
        P(("rep", "fsdp"), None),
        P(("rep", "fsdp"), None),
        P(("rep", "fsdp")),
        P(("rep", "fsdp"), None, None),
        P("fsdp"),
        P("fsdp", None),
        P("fsdp", None),
        P("fsdp", None),
        P("fsdp", None),
        P("fsdp"),
        P("fsdp", None),
        P("fsdp", None),
        P("fsdp", None),
    )
    out_specs = (
        P(("rep", "fsdp"), None),
        P(("rep", "fsdp"), None),
        P("fsdp"),
        P("fsdp", None),
        P("fsdp", None),
        P("fsdp", None),
        P("fsdp", None),
        P("fsdp"),
        P("fsdp", None),
        P("fsdp", None),
        P("fsdp", None),
    )
    return jax.shard_map(body, mesh=mesh, in_specs=in_specs, out_specs=out_specs, check_vma=False)
```

profile of v0, /device:TPU:0, one launch (start us, length us, event | category | flops | bytes accessed | tf_op | source)
XLA Modules:
  0.0 1064.0 jit_solution(13431715614173983107)
XLA Ops:
  18.7 18.8 %all-reduce.5 = (bf16[768]{0:T(1024)(128)(2,1)S(1)}, bf16[768]{0:T(1024)(128)(2,1)}) all-reduce(bf16[768]{0:T(1024)(128)(2,1)S(1)} %dynamic-update-slice, bf16[768]{0:T(1024)(128)(2,1)S(1)} %dynamic-update-slice.1), channel_id=1, replica_groups=mesh['rep'=4,'fsdp'=8] {'fsdp'}, use_global_device_ids=true, to_apply=%add | all-reduce | flops 1536 | bytes 6144
  44.3 5.8 copy.103
  54.9 6.7 fusion.87
  61.7 10.4 reshape.201
  72.1 6.7 fusion.89
  78.8 10.4 reshape.199
  89.2 8.6 subtract_convert_fusion.2
  108.4 5.9 convolution_convert_fusion.1
  114.3 5.8 copy.99
  120.1 9.1 convert_element_type.168
  136.5 96.6 %while.28 = (s32[]{:T(128)}, bf16[12,4,576,64]{2,3,1,0:T(8,128)(2,1)}, f32[12,4,576]{2,1,0:T(4,128)}, bf16[12,4,576,64]{2,3,1,0:T(8,128)(2,1)}, bf16[12,4,576,64...) while((s32[]{:T(128)}, bf16[12,4,576,64]{2,3,1,0:T(8,128)(2,1)}, ...), condition=%wide.region_4.5_spmd.clone, body=%wide.region_1.4_spmd.clone.sunk | while | flops 356140800 | bytes 18639960 | solution.py:136
  233.2 7.0 copy.139
  240.2 8.0 reshape.205
  248.2 5.8 multiply_reduce_fusion.3
  259.4 12.5 %fusion.92 = f32[2304,2048]{1,0:T(8,128)} fusion(bf16[2304,768]{0,1:T(8,128)(2,1)S(1)} %multiply_convert_fusion.5, bf16[768,2048]{1,0:T(8,128)(2,1)} %all-gather.16.cloned.1.call-done), kind=kOutput, calls=%fused_computation.143 | convolution fusion | flops 7247757312 | bytes 25559040 | tf_op jit(solution)/shard_map/dot_general | solution.py:149
  271.9 14.0 %fusion.93 = f32[2304,2048]{1,0:T(8,128)} fusion(bf16[2304,768]{0,1:T(8,128)(2,1)} %copy-done.6, bf16[768,2048]{1,0:T(8,128)(2,1)} %all-gather.18.cloned.1.call-done), kind=kOutput, calls=%fused_computation.144 | convolution fusion | flops 7247757312 | bytes 25559040 | tf_op jit(solution)/shard_map/dot_general | solution.py:150
  286.0 29.0 %multiply_convert_fusion.1 = (bf16[2304,2048]{1,0:T(8,128)(2,1)}, bf16[2304,2048]{1,0:T(8,128)(2,1)}, bf16[2304,2048]{1,0:T(8,128)(2,1)}) fusion(f32[2304,2048]{1,0:T(8,128)} %fusion.92, f32[2304,2048]{1,0:T(8,128)} %fusion.93, bf16[2048,768]{1,0:T(8,128)(2,1)} %all-gather.20.cloned.1.call-done, bf16[2304,768]{0,1:T(8,128)(2,1)S(1)} %copy-done.4, ...), kind=kOutput, calls=%fused_computation.64 | convolution fusion | flops 7328563200 | bytes 72754176 | tf_op jit(solution)/shard_map/dot_general | solution.py:22
  315.0 12.7 %fusion.94 = f32[2304,768]{0,1:T(8,128)} fusion(bf16[2304,2048]{1,0:T(8,128)(2,1)} %get-tuple-element.238, bf16[768,2048]{1,0:T(8,128)(2,1)S(1)} %copy-done.23), kind=kOutput, calls=%fused_computation.145 | convolution fusion | flops 7247757312 | bytes 19660800 | tf_op jit(solution)/shard_map/dot_general | solution.py:22
  327.7 16.7 %multiply_reduce_fusion.1 = (f32[768]{0:T(1024)}, f32[2304]{0:T(1024)S(1)}, f32[2304,768]{0,1:T(8,128)S(1)}) fusion(f32[2304,768]{0,1:T(8,128)} %copy-done.3, f32[2304]{0:T(1024)S(1)} %get-tuple-element.260, f32[768]{0:T(1024)S(1)} %copy-done.15, f32[2304,768]{0,1:T(8,128)} %fusion.94, bf16[2304,2048]{1,0:T(8,128)(2,1)} %get-tuple-element.237, ...), kind=kOutput, calls=%fused_computation.88 | convolution fusion | flops 7260140544 | bytes 33841152 | tf_op jit(solution)/shard_map/dot_general | solution.py:22
  358.6 5.7 reshape.206
  371.5 198.3 %while.29 = (s32[]{:T(128)}, f32[12,4,576,64]{2,3,1,0:T(8,128)}, f32[12,4,576,64]{2,3,1,0:T(8,128)}, bf16[12,4,576,64]{2,3,1,0:T(8,128)(2,1)}, bf16[12,4,576,64]...) while((s32[]{:T(128)}, f32[12,4,576,64]{2,3,1,0:T(8,128)}, ...), condition=%wide.region_9.10_spmd.clone, body=%wide.region_7.9_spmd.clone.sunk | while | flops 870024960 | bytes 45142128 | solution.py:227
  569.8 8.3 copy.136
  578.1 11.5 %copy.137 = f32[4,12,576,64]{2,0,3,1:T(4,128)} copy(f32[4,12,576,64]{2,3,1,0:T(8,128)} %bitcast.187) | data formatting | bytes 14155776 | tf_op jit(solution)/shard_map/reshape | solution.py:70
  589.6 8.1 subtract_convert_fusion
  602.1 8.0 convert_element_type.179
  610.1 6.4 fusion.84
  616.6 6.6 pad_maximum_fusion.1
  623.2 8.0 convert_element_type.180
  631.2 6.4 fusion.82
  637.6 7.1 copy.138
  644.7 7.8 reshape.211
  652.5 6.4 fusion.80
  659.0 8.4 fusion.75
  667.5 13.1 %fusion.95 = f32[768,2048]{1,0:T(8,128)} fusion(bf16[2304,768]{0,1:T(8,128)(2,1)} %copy-done.6, bf16[2304,2048]{1,0:T(8,128)(2,1)} %get-tuple-element.238), kind=kOutput, calls=%fused_computation.146 | convolution fusion | flops 7247757312 | bytes 19267584 | tf_op jit(solution)/shard_map/dot_general | solution.py:16
  680.7 12.8 %fusion.96 = f32[768,2048]{1,0:T(8,128)} fusion(bf16[2304,768]{0,1:T(8,128)(2,1)} %copy-done.6, bf16[2304,2048]{1,0:T(8,128)(2,1)} %get-tuple-element.237), kind=kOutput, calls=%fused_computation.147 | convolution fusion | flops 7247757312 | bytes 19267584 | tf_op jit(solution)/shard_map/dot_general | solution.py:16
  693.6 13.1 %fusion.71 = f32[2048,768]{1,0:T(8,128)} fusion(bf16[2304,2048]{1,0:T(8,128)(2,1)} %get-tuple-element.239, bf16[2304,768]{0,1:T(8,128)(2,1)} %copy.103, f32[2304]{0:T(1024)} %reshape.212), kind=kOutput, calls=%fused_computation.112 | convolution fusion | flops 7253065728 | bytes 19276800 | tf_op jit(solution)/shard_map/dot_general | solution.py:16
  707.4 8.3 fusion.97
  720.9 13.8 %add_convert_fusion = bf16[2304,768]{0,1:T(8,128)(2,1)} fusion(f32[2304,768]{0,1:T(8,128)} %copy-done.3, bf16[2304,2048]{1,0:T(8,128)(2,1)} %get-tuple-element.239, bf16[2048,768]{1,0:T(8,128)(2,1)S(1)} %copy-done.22, f32[2304]{0:T(1024)S(1)} %copy-done.19), kind=kOutput, calls=%fused_computation.92 | convolution fusion | flops 7253065728 | bytes 23208960 | tf_op jit(solution)/shard_map/dot_general | solution.py:154
  739.6 25.2 %reduce-scatter.14.cloned.1.call-done = f32[96,768]{1,0:T(8,128)} async-done(((f32[768,768]{1,0:T(8,128)}), f32[96,768]{1,0:T(8,128)}) %reduce-scatter.14.cloned.1.call-update) | async-done | bytes 294928 | tf_op jit(solution)/shard_map/reduce_scatter | solution.py:258
  766.4 69.3 %reduce-scatter.16.cloned.1.call-done = f32[96,2048]{1,0:T(8,128)} async-done(((f32[768,2048]{1,0:T(8,128)}), f32[96,2048]{1,0:T(8,128)}) %reduce-scatter.16.cloned.1.call-update) | async-done | bytes 786448 | tf_op jit(solution)/shard_map/reduce_scatter | solution.py:180
  837.7 68.6 %reduce-scatter.18.cloned.1.call-done = f32[96,2048]{1,0:T(8,128)} async-done(((f32[768,2048]{1,0:T(8,128)}), f32[96,2048]{1,0:T(8,128)}) %reduce-scatter.18.cloned.1.call-update) | async-done | bytes 786448 | tf_op jit(solution)/shard_map/reduce_scatter | solution.py:181
  908.2 68.4 %reduce-scatter.20.cloned.1.call-done = f32[256,768]{1,0:T(8,128)} async-done(((f32[2048,768]{1,0:T(8,128)}), f32[256,768]{1,0:T(8,128)}) %reduce-scatter.20.cloned.1.call-update) | async-done | bytes 786448 | tf_op jit(solution)/shard_map/reduce_scatter | solution.py:182
  978.6 13.7 %fusion.70 = (f32[768]{0:T(1024)}, f32[2304]{0:T(1024)}, f32[2304,768]{0,1:T(8,128)}) fusion(bf16[2304,768]{0,1:T(8,128)(2,1)S(1)} %copy-done.1, f32[2304]{0:T(1024)S(1)} %copy-done.11, f32[768]{0:T(1024)S(1)} %copy-done.13, bf16[768,768]{1,0:T(8,128)(2,1)} %all-gather.12.cloned.1.call-done, bf16[2304,768]{0,1:T(8,128)(2,1)} %reshape.211, ...), kind=kOutput, calls=%fused_computation.87 | convolution fusion | flops 2733831168 | bytes 29515776 | tf_op jit(solution)/shard_map/dot_general | solution.py:22
  992.3 5.8 copy.114
  998.8 8.0 fusion.67
  1006.8 8.0 copy.115
  1014.8 14.1 %all-reduce.4 = (bf16[768]{0:T(1024)(128)(2,1)S(1)}, bf16[768]{0:T(1024)(128)(2,1)S(1)}) all-reduce(f32[768]{0:T(1024)S(1)} %copy-done.16, f32[768]{0:T(1024)S(1)} %copy-done.20), channel_id=2, replica_groups=mesh['rep'=4,'fsdp'=8] {'fsdp'}, use_global_device_ids=true, to_apply=%region_12.13.clone | all-reduce | flops 1536 | bytes 9216
  1029.1 10.1 all-reduce.6
  (314 shorter events, 402.3 us)
Async XLA Ops:
  7.2 47.7 %all-gather.10.cloned.1.call-start = ((), (), s32[]{:S(2)}) async-start(), calls=%async_computation.8 | async-start | bytes 1327104 | tf_op jit(solution)/shard_map/all_gather | solution.py:103
  7.9 64.1 %all-gather.8.cloned.1.call-start = ((), (), s32[]{:S(2)}) async-start(), calls=%async_computation.7 | async-start | bytes 1327104 | tf_op jit(solution)/shard_map/all_gather | solution.py:102
  8.7 99.7 %all-gather.12.cloned.1.call-start = ((), (), s32[]{:S(2)}) async-start(), calls=%async_computation.9 | async-start | bytes 1327104 | tf_op jit(solution)/shard_map/all_gather | solution.py:104
  9.4 238.8 %all-gather.14.cloned.1.call-start = ((), (), s32[]{:S(2)}) async-start(), calls=%async_computation.10 | async-start | bytes 1327104 | tf_op jit(solution)/shard_map/all_gather | solution.py:105
  10.0 247.7 %all-gather.16.cloned.1.call-start = ((), (), s32[]{:S(2)}) async-start(), calls=%async_computation.11 | async-start | bytes 3538944 | tf_op jit(solution)/shard_map/all_gather | solution.py:143
  10.6 6.3 copy-start.21
  10.6 7.7 copy-start.26
  10.6 7.9 copy-start.27
  10.6 261.3 %all-gather.18.cloned.1.call-start = ((), (), s32[]{:S(2)}) async-start(), calls=%async_computation.12 | async-start | bytes 3538944 | tf_op jit(solution)/shard_map/all_gather | solution.py:144
  11.2 274.8 %all-gather.20.cloned.1.call-start = ((), (), s32[]{:S(2)}) async-start(), calls=%async_computation.13 | async-start | bytes 3538944 | tf_op jit(solution)/shard_map/all_gather | solution.py:145
  11.9 722.7 %reduce-scatter.8.cloned.1.call-start = ((), (), s32[]{:S(2)}) async-start(), calls=%async_computation.14 | async-start | bytes 2654208 | tf_op jit(solution)/shard_map/reduce_scatter | solution.py:255
  16.8 231.4 %copy-start = (bf16[2304,768]{0,1:T(8,128)(2,1)}, bf16[2304,768]{0,1:T(8,128)(2,1)S(1)}, u32[]{:S(2)}) copy-start(bf16[2304,768]{0,1:T(8,128)(2,1)S(1)} %copy.94) | copy-start | bytes 10616836
  37.5 70.9 %copy-start.12 = (f32[768]{0:T(1024)}, f32[768]{0:T(1024)S(1)}, u32[]{:S(2)}) copy-start(f32[768]{0:T(1024)S(1)} %convert_element_type.161) | copy-start | bytes 9220
  38.9 69.5 %copy-start.10 = (f32[2304]{0:T(1024)}, f32[2304]{0:T(1024)S(1)}, u32[]{:S(2)}) copy-start(f32[2304]{0:T(1024)S(1)} %get-tuple-element.258) | copy-start | bytes 27652
  240.2 8.0 copy-start.17
  248.2 8.8 copy-start.15
  254.0 3.0 copy-start.3
  257.6 1.8 copy-start.6
  271.9 14.0 %copy-start.4 = (bf16[2304,768]{0,1:T(8,128)(2,1)S(1)}, bf16[2304,768]{0,1:T(8,128)(2,1)}, u32[]{:S(2)}) copy-start(bf16[2304,768]{0,1:T(8,128)(2,1)} %copy.103) | copy-start | bytes 10616836
  286.0 29.0 %copy-start.23 = (bf16[768,2048]{1,0:T(8,128)(2,1)S(1)}, bf16[768,2048]{1,0:T(8,128)(2,1)}, u32[]{:S(2)}) copy-start(bf16[768,2048]{1,0:T(8,128)(2,1)} %all-gather.16.cloned.1.call-done) | copy-start | bytes 9437188
  327.7 16.7 %slice-start = ((s8[7077888]{0:T(1024)(128)(4,1)}), s8[4194304]{0:T(1024)(128)(4,1)S(1)}, s32[]{:S(2)}) async-start(s8[7077888]{0:T(1024)(128)(4,1)} %bitcast.175), calls=%async_computation.22 | async-start | bytes 8388608
  327.7 16.7 %slice-start.1 = ((s8[7077888]{0:T(1024)(128)(4,1)}), s8[2883584]{0:T(1024)(128)(4,1)S(1)}, s32[]{:S(2)}) async-start(s8[7077888]{0:T(1024)(128)(4,1)} %bitcast.175), calls=%async_computation.23 | async-start | bytes 5767168
  327.7 16.7 %copy-start.14 = (f32[2304]{0:T(1024)S(1)}, f32[2304]{0:T(1024)}, u32[]{:S(2)}) copy-start(f32[2304]{0:T(1024)} %get-tuple-element.259) | copy-start | bytes 27652
  344.4 5.3 copy-start.18
  344.4 5.3 copy-start.25
  346.8 2.9 copy-start.2
  578.1 11.5 %copy-start.7 = (f32[4,576,32]{1,0,2:T(4,128)S(1)}, f32[4,576,32]{1,0,2:T(4,128)}, u32[]{:S(2)}) copy-start(f32[4,576,32]{1,0,2:T(4,128)} %get-tuple-element.254) | copy-start | bytes 884740
  578.1 11.5 %copy-start.8 = (f32[4,576,32]{1,0,2:T(4,128)S(1)}, f32[4,576,32]{1,0,2:T(4,128)}, u32[]{:S(2)}) copy-start(f32[4,576,32]{1,0,2:T(4,128)} %get-tuple-element.252) | copy-start | bytes 884740
  602.1 8.0 copy-start.1
  602.1 8.0 copy-start.11
  602.1 8.0 copy-start.13
  616.5 119.7 %reduce-scatter.10.cloned.1.call-start = ((), (), s32[]{:S(2)}) async-start(), calls=%async_computation.15 | async-start | bytes 2654208 | tf_op jit(solution)/shard_map/reduce_scatter | solution.py:256
  637.6 100.3 %reduce-scatter.12.cloned.1.call-start = ((), (), s32[]{:S(2)}) async-start(), calls=%async_computation.16 | async-start | bytes 2654208 | tf_op jit(solution)/shard_map/reduce_scatter | solution.py:257
  658.9 105.9 %reduce-scatter.14.cloned.1.call-start = ((), (), s32[]{:S(2)}) async-start(), calls=%async_computation.17 | async-start | bytes 2654208 | tf_op jit(solution)/shard_map/reduce_scatter | solution.py:258
  667.4 168.3 %reduce-scatter.16.cloned.1.call-start = ((), (), s32[]{:S(2)}) async-start(), calls=%async_computation.18 | async-start | bytes 7077888 | tf_op jit(solution)/shard_map/reduce_scatter | solution.py:180
  680.6 225.7 %reduce-scatter.18.cloned.1.call-start = ((), (), s32[]{:S(2)}) async-start(), calls=%async_computation.19 | async-start | bytes 7077888 | tf_op jit(solution)/shard_map/reduce_scatter | solution.py:181
  693.5 283.1 %reduce-scatter.20.cloned.1.call-start = ((), (), s32[]{:S(2)}) async-start(), calls=%async_computation.20 | async-start | bytes 7077888 | tf_op jit(solution)/shard_map/reduce_scatter | solution.py:182
  706.7 338.9 %all-reduce.10.cloned.1.call-start = ((), (), s32[]{:S(2)}) async-start(), calls=%async_computation.21 | async-start | bytes 3538944 | tf_op jit(solution)/shard_map/psum | solution.py:262
  707.4 8.3 copy-start.5
  707.4 8.3 copy-start.24
  715.7 5.2 copy-start.19
  715.7 5.2 copy-start.22
  1006.8 8.0 copy-start.16
  1006.8 8.0 copy-start.20
  1045.6 10.5 copy-start.9
Sparse Core Ops, SparseCore 0:
  9.7 25.5 all-gather.9
  36.9 22.3 all-gather.7
  60.9 22.4 all-gather.11
  84.9 22.4 all-gather.13
  108.8 38.0 all-gather.15
  148.4 37.1 all-gather.17
  187.2 37.1 all-gather.19
  616.7 34.4 reduce-scatter.7
  653.5 35.7 reduce-scatter.9
  691.5 35.4 reduce-scatter.11
  729.3 35.4 reduce-scatter.13
  767.0 68.7 reduce-scatter.15
  838.1 68.1 reduce-scatter.17
  908.5 68.1 reduce-scatter.19
  981.6 63.9 all-reduce.9
where the time goes:
time: 1080 us; the launch traced here: 1060 us
  matrix products  461 us (43%)
  waiting for transfers between devices  242 us (22%)
  local copies, waits for them, and re-layouts  174 us (16%)
  other arithmetic  127 us (12%)
  blocking collectives  43 us (4%)
  between operations  16.1 us (1%)
    dot_general x7, matrix products, through(): lax.dot_general(left, right, (((1,), (1,)), ((), ())), preferred_element_...  90.1 us
    reduce_scatter x1, waiting for transfers between devices, body(): lax.psum_scatter(grad_gate, 'fsdp', scatter_dimension=0, tiled=True)  69.3 us
    reduce_scatter x1, waiting for transfers between devices, body(): lax.psum_scatter(grad_up, 'fsdp', scatter_dimension=0, tiled=True)  68.6 us
    reduce_scatter x1, waiting for transfers between devices, body(): lax.psum_scatter(grad_down, 'fsdp', scatter_dimension=0, tiled=True)  68.4 us
    dot_general x7, matrix products, across(): lax.dot_general(left, right, (((0,), (0,)), ((), ())), preferred_element_...  66.6 us
    dot_general x24, matrix products, block_scores(): jnp.einsum('hqd,hkd->hqk', query_block, key_block, preferred_element_type...  52.4 us
    dot_general x12, matrix products, attend(): jnp.einsum('hqk,hkd->hqd', probs_low, member[2], preferred_element_type=j...  44 us
    dot_general x12, matrix products, attend_back(): jnp.einsum('hqk,hqd->hkd', attn_probs.astype(jnp.bfloat16), grad_block, p...  41 us
  transfers between devices with their start and end apart: 15, of which 5 were waited for; matrix products, arithmetic and copies ran while one was open for 39% of the time, Pallas kernels for 0%

commit v1 on v0

v1 whole, which is shorter than its diff:
```python
import functools
import jax
import jax.numpy as jnp
import numpy as np
from jax import lax
from jax.experimental import pallas as pl
from jax.experimental.pallas import tpu as pltpu
from jax.sharding import PartitionSpec as P

HEAD_DIM = 64
COLS = 24
EPSILON = 1e-05
GROUP = 4
GW = GROUP * HEAD_DIM
HALF = GW // 2
BF = jnp.bfloat16
F32 = jnp.float32


def nn(a, b):
    return lax.dot_general(a, b, (((1,), (0,)), ((), ())), preferred_element_type=F32)


def nt(a, b):
    return lax.dot_general(a, b, (((1,), (1,)), ((), ())), preferred_element_type=F32)


def tn(a, b):
    return lax.dot_general(a, b, (((0,), (0,)), ((), ())), preferred_element_type=F32)


def params(limit=60):
    return pltpu.CompilerParams(vmem_limit_bytes=limit * 1024 * 1024)


def norm_kernel(x_ref, gain_ref, out_ref):
    x = x_ref[...].astype(F32)
    inv = lax.rsqrt(jnp.mean(x * x, axis=-1, keepdims=True) + EPSILON)
    out_ref[...] = (x * inv * gain_ref[...]).astype(BF)


def norm_call(x, gain, rows):
    n, d = x.shape
    return pl.pallas_call(
        norm_kernel,
        grid=(n // rows,),
        in_specs=[pl.BlockSpec((rows, d), lambda i: (i, 0)), pl.BlockSpec((1, d), lambda i: (0, 0))],
        out_specs=pl.BlockSpec((rows, d), lambda i: (i, 0)),
        out_shape=jax.ShapeDtypeStruct((n, d), BF),
        compiler_params=params(),
        name="norm_in",
    )(x, gain)


def head_masks():
    lane = lax.broadcasted_iota(jnp.int32, (1, GW), 1)
    rot = [((lane % HALF) // (HEAD_DIM // 2) == h) for h in range(GROUP)]
    nat = [(lane // HEAD_DIM == h) for h in range(GROUP)]
    return rot, nat


def mask_to(x, m):
    return x * jnp.where(m, 1.0, 0.0).astype(x.dtype)


def blocks_of(total, size):
    return [(s, min(s + size, total)) for s in range(0, total, size)]


def attn_fwd_kernel(slot, size, nm_ref, w_ref, cos_ref, sin_ref, qkv_ref, att_ref, lse_ref):
    nm = nm_ref[...]
    cos = cos_ref[...]
    sin = sin_ref[...]
    rot_m, nat_m = head_masks()

    def rotated(lo, scale):
        u = nn(nm, w_ref[:, lo : lo + GW])
        a, b = u[:, :HALF], u[:, HALF:]
        r = jnp.concatenate([a * cos - b * sin, a * sin + b * cos], axis=1)
        return r.astype(BF) * jnp.asarray(scale, BF)

    q = rotated(0, HEAD_DIM ** (-0.5))
    k = rotated(GW, 1.0)
    v = nn(nm, w_ref[:, 2 * GW :]).astype(BF)
    qkv_ref[:, :GW] = q
    qkv_ref[:, GW : 2 * GW] = k
    qkv_ref[:, 2 * GW :] = v
    qs = [mask_to(q, m) for m in rot_m]
    vs = [mask_to(v, m) for m in nat_m]
    lane = lax.broadcasted_iota(jnp.int32, (1, 128), 1)
    for s, e in blocks_of(slot, size):
        row = lax.broadcasted_iota(jnp.int32, (e - s, e - s), 0)
        col = lax.broadcasted_iota(jnp.int32, (e - s, e - s), 1)
        causal = row >= col
        out = None
        logs = jnp.zeros((e - s, 128), F32)
        for h in range(GROUP):
            qh = qs[h][s:e]
            diag = jnp.where(causal, nt(qh, k[s:e]), -1e30)
            top = jnp.max(diag, axis=-1, keepdims=True)
            if s:
                left = nt(qh, k[:s])
                top = jnp.maximum(top, jnp.max(left, axis=-1, keepdims=True))
            pd = jnp.exp(diag - top)
            total = jnp.sum(pd, axis=-1, keepdims=True)
            o = nn(pd.astype(BF), vs[h][s:e])
            if s:
                pleft = jnp.exp(left - top)
                total = total + jnp.sum(pleft, axis=-1, keepdims=True)
                o = o + nn(pleft.astype(BF), vs[h][:s])
            o = o * (1.0 / total)
            out = o if out is None else out + o
            logs = jnp.where(lane == h, top + jnp.log(total), logs)
        att_ref[s:e, :] = out.astype(BF)
        lse_ref[0, 0, :, s:e] = logs.T[:8]


def attn_fwd(nm, w, cos, sin, slot, size=256):
    n, d = nm.shape
    crops = n // slot
    groups = w.shape[1] // (3 * GW)
    return pl.pallas_call(
        functools.partial(attn_fwd_kernel, slot, size),
        grid=(groups, crops),
        in_specs=[
            pl.BlockSpec((slot, d), lambda g, c: (c, 0)),
            pl.BlockSpec((d, 3 * GW), lambda g, c: (0, g)),
            pl.BlockSpec((slot, HALF), lambda g, c: (c, 0)),
            pl.BlockSpec((slot, HALF), lambda g, c: (c, 0)),
        ],
        out_specs=[
            pl.BlockSpec((slot, 3 * GW), lambda g, c: (c, g)),
            pl.BlockSpec((slot, GW), lambda g, c: (c, g)),
            pl.BlockSpec((1, 1, 8, slot), lambda g, c: (g, c, 0, 0)),
        ],
        out_shape=[
            jax.ShapeDtypeStruct((n, groups * 3 * GW), BF),
            jax.ShapeDtypeStruct((n, groups * GW), BF),
            jax.ShapeDtypeStruct((groups, crops, 8, slot), F32),
        ],
        compiler_params=params(),
        name="attn_fwd",
    )(nm, w, cos, sin)


def attn_bwd_kernel(slot, size, qkv_ref, go_ref, att_ref, lse_ref, nm_ref, cos_ref, sin_ref,
                    gqkv_ref, dw_ref, dst_ref, dq_ref, acc_ref):
    crop = pl.program_id(1)
    q = qkv_ref[:, :GW]
    k = qkv_ref[:, GW : 2 * GW]
    v = qkv_ref[:, 2 * GW :]
    go = go_ref[...]
    rot_m, nat_m = head_masks()
    prod = go.astype(F32) * att_ref[...].astype(F32)
    hi = prod.astype(BF)
    lo = (prod - hi.astype(F32)).astype(BF)
    pick = (
        lax.broadcasted_iota(jnp.int32, (8, GW), 1) // HEAD_DIM
        == lax.broadcasted_iota(jnp.int32, (8, GW), 0)
    )
    pick = jnp.where(pick, 1.0, 0.0).astype(BF)
    delta = nt(pick, hi) + nt(pick, lo)
    blocks = blocks_of(slot, size)
    dk = [None] * len(blocks)
    dv = [None] * len(blocks)
    for h in range(GROUP):
        qm = mask_to(q, rot_m[h])
        km = mask_to(k, rot_m[h])
        gm = mask_to(go, nat_m[h])
        for j, (s, e) in enumerate(blocks):
            w = e - s
            row = lax.broadcasted_iota(jnp.int32, (w, w), 0)
            col = lax.broadcasted_iota(jnp.int32, (w, w), 1)
            parts = [(s, e, True)] + ([(e, slot, False)] if e < slot else [])
            for ps, pe, diag in parts:
                sc = nt(k[s:e], qm[ps:pe])
                p = jnp.exp(sc - lse_ref[0, 0, h : h + 1, ps:pe])
                if diag:
                    p = jnp.where(col >= row, p, 0.0)
                dp = nt(v[s:e], gm[ps:pe])
                ds = (p * (dp - delta[h : h + 1, ps:pe])).astype(BF)
                dst_ref[s:e, ps:pe] = ds
                dvp = nn(p.astype(BF), gm[ps:pe])
                dkp = nn(ds, qm[ps:pe])
                dv[j] = dvp if dv[j] is None else dv[j] + dvp
                dk[j] = dkp if dk[j] is None else dk[j] + dkp
        for s, e in blocks:
            part = tn(dst_ref[:e, s:e], km[:e])
            if h:
                dq_ref[s:e] += part
            else:
                dq_ref[s:e] = part
    cos = cos_ref[...]
    sin = sin_ref[...]

    def back(u, c, t):
        a, b = u[:, :HALF], u[:, HALF:]
        return jnp.concatenate([a * c + b * t, b * c - a * t], axis=1).astype(BF)

    for j, (s, e) in enumerate(blocks):
        c, t = cos[s:e], sin[s:e]
        gqkv_ref[s:e, :GW] = back(dq_ref[s:e] * (HEAD_DIM ** (-0.5)), c, t)
        gqkv_ref[s:e, GW : 2 * GW] = back(dk[j], c, t)
        gqkv_ref[s:e, 2 * GW :] = dv[j].astype(BF)
    part = tn(nm_ref[...], gqkv_ref[...])

    @pl.when(crop == 0)
    def _():
        acc_ref[...] = part

    @pl.when(crop != 0)
    def _():
        acc_ref[...] += part

    @pl.when(crop == pl.num_programs(1) - 1)
    def _():
        dw_ref[...] = acc_ref[...].astype(BF)


def attn_bwd(qkv, go, att, lse, nm, cos, sin, slot, size=256):
    n, d = nm.shape
    crops = n // slot
    groups = lse.shape[0]
    row_spec = lambda w: pl.BlockSpec((slot, w), lambda g, c: (c, g))
    crop_spec = lambda w: pl.BlockSpec((slot, w), lambda g, c: (c, 0))
    return pl.pallas_call(
        functools.partial(attn_bwd_kernel, slot, size),
        grid=(groups, crops),
        in_specs=[
            row_spec(3 * GW),
            row_spec(GW),
            row_spec(GW),
            pl.BlockSpec((1, 1, 8, slot), lambda g, c: (g, c, 0, 0)),
            crop_spec(d),
            crop_spec(HALF),
            crop_spec(HALF),
        ],
        out_specs=[row_spec(3 * GW), pl.BlockSpec((d, 3 * GW), lambda g, c: (0, g))],
        out_shape=[
            jax.ShapeDtypeStruct((n, groups * 3 * GW), BF),
            jax.ShapeDtypeStruct((d, groups * 3 * GW), BF),
        ],
        scratch_shapes=[
            pltpu.VMEM((slot, slot), BF),
            pltpu.VMEM((slot, GW), F32),
            pltpu.VMEM((d, 3 * GW), F32),
        ],
        compiler_params=params(),
        name="attn_bwd",
    )(qkv, go, att, lse, nm, cos, sin)


def valid_rows(heights_ref, c, slot):
    return lax.broadcasted_iota(jnp.int32, (slot, 1), 0) < heights_ref[c] * COLS


def out_proj_kernel(slot, heights_ref, x_ref, att_ref, wo_ref, gain_ref, mid_ref, nm_ref):
    valid = valid_rows(heights_ref, pl.program_id(0), slot)
    proj = nn(att_ref[...], wo_ref[...])
    mid = x_ref[...].astype(F32) + jnp.where(valid, proj, 0.0)
    mid_ref[...] = mid
    inv = lax.rsqrt(jnp.mean(mid * mid, axis=-1, keepdims=True) + EPSILON)
    nm_ref[...] = (mid * inv * gain_ref[...]).astype(BF)


def out_proj(heights, x, att, wo, gain, slot):
    n, d = x.shape
    rows = pl.BlockSpec((slot, d), lambda c, *_: (c, 0))
    return pl.pallas_call(
        functools.partial(out_proj_kernel, slot),
        grid_spec=pltpu.PrefetchScalarGridSpec(
            num_scalar_prefetch=1,
            grid=(n // slot,),
            in_specs=[
                rows,
                rows,
                pl.BlockSpec((d, d), lambda c, *_: (0, 0)),
                pl.BlockSpec((1, d), lambda c, *_: (0, 0)),
            ],
            out_specs=[rows, rows],
        ),
        out_shape=[jax.ShapeDtypeStruct((n, d), F32), jax.ShapeDtypeStruct((n, d), BF)],
        compiler_params=params(),
        name="out_proj",
    )(heights, x, att, wo, gain)


def mlp_kernel(slot, heights_ref, nm_ref, cot_ref, mid_ref, wg_ref, wu_ref, wd_ref,
               out_ref, dn_ref, dwg_ref, dwu_ref, dwd_ref,
               nmt_ref, gbt_ref, oacc_ref, dacc_ref, ag_ref, au_ref, ad_ref):
    f = pl.program_id(0)
    c = pl.program_id(1)
    last_f = pl.num_programs(0) - 1
    last_c = pl.num_programs(1) - 1
    valid = valid_rows(heights_ref, c, slot)
    nm = nm_ref[...]
    gb = jnp.where(valid, cot_ref[...], jnp.zeros((), BF))

    @pl.when(f == 0)
    def _():
        nmt_ref[c] = nm.T
        gbt_ref[c] = gb.T

    g = nn(nm, wg_ref[...])
    u = nn(nm, wu_ref[...])
    gh = nt(gb, wd_ref[...])
    sg = 1.0 / (1.0 + jnp.exp(-g))
    act = g * sg
    hid = (act * u).astype(BF)
    gu = (gh * act).astype(BF)
    gg = (gh * u * (sg * (1.0 + g * (1.0 - sg)))).astype(BF)
    o = nn(hid, wd_ref[...])
    dn = nt(gg, wg_ref[...]) + nt(gu, wu_ref[...])
    nmt = nmt_ref[c]
    dg = nn(nmt, gg)
    du = nn(nmt, gu)
    dd = nn(gbt_ref[c], hid)

    @pl.when(f == 0)
    def _():
        oacc_ref[c] = o
        dacc_ref[c] = dn

    @pl.when(f != 0)
    def _():
        oacc_ref[c] += o
        dacc_ref[c] += dn

    @pl.when(c == 0)
    def _():
        ag_ref[...] = dg
        au_ref[...] = du
        ad_ref[...] = dd

    @pl.when(c != 0)
    def _():
        ag_ref[...] += dg
        au_ref[...] += du
        ad_ref[...] += dd

    @pl.when(c == last_c)
    def _():
        dwg_ref[...] = ag_ref[...].astype(BF)
        dwu_ref[...] = au_ref[...].astype(BF)
        dwd_ref[...] = ad_ref[...].astype(BF).T

    @pl.when(f == last_f)
    def _():
        out_ref[...] = (mid_ref[...] + jnp.where(valid, oacc_ref[c], 0.0)).astype(BF)
        dn_ref[...] = dacc_ref[c]


def mlp(heights, nm, cot, mid, wg, wu, wd, slot, chunk=512):
    n, d = nm.shape
    crops = n // slot
    ff = wg.shape[1]
    nf = ff // chunk

    def last(f, c, *_):
        return (jnp.where(f == nf - 1, c, 0), 0)

    every = pl.BlockSpec((slot, d), lambda f, c, *_: (c, 0))
    wide = pl.BlockSpec((d, chunk), lambda f, c, *_: (0, f))
    tall = pl.BlockSpec((chunk, d), lambda f, c, *_: (f, 0))
    return pl.pallas_call(
        functools.partial(mlp_kernel, slot),
        grid_spec=pltpu.PrefetchScalarGridSpec(
            num_scalar_prefetch=1,
            grid=(nf, crops),
            in_specs=[every, every, pl.BlockSpec((slot, d), last), wide, wide, tall],
            out_specs=[pl.BlockSpec((slot, d), last), pl.BlockSpec((slot, d), last), wide, wide, tall],
            scratch_shapes=[
                pltpu.VMEM((crops, d, slot), BF),
                pltpu.VMEM((crops, d, slot), BF),
                pltpu.VMEM((crops, slot, d), F32),
                pltpu.VMEM((crops, slot, d), F32),
                pltpu.VMEM((d, chunk), F32),
                pltpu.VMEM((d, chunk), F32),
                pltpu.VMEM((d, chunk), F32),
            ],
        ),
        out_shape=[
            jax.ShapeDtypeStruct((n, d), BF),
            jax.ShapeDtypeStruct((n, d), F32),
            jax.ShapeDtypeStruct((d, ff), BF),
            jax.ShapeDtypeStruct((d, ff), BF),
            jax.ShapeDtypeStruct((ff, d), BF),
        ],
        compiler_params=params(),
        name="mlp",
    )(heights, nm, cot, mid, wg, wu, wd)


def mid_grad_kernel(slot, heights_ref, cot_ref, mid_ref, dn_ref, gain_ref, wo_ref, att_ref,
                    gmid_ref, gatt_ref, dwo_ref, acc_ref):
    c = pl.program_id(0)
    valid = valid_rows(heights_ref, c, slot)
    mid = mid_ref[...]
    inv = lax.rsqrt(jnp.mean(mid * mid, axis=-1, keepdims=True) + EPSILON)
    e = dn_ref[...] * gain_ref[...]
    gm = (
        cot_ref[...].astype(F32)
        + inv * e
        - mid * (inv * inv * inv * jnp.mean(e * mid, axis=-1, keepdims=True))
    )
    gmid_ref[...] = gm
    ga = jnp.where(valid, gm, 0.0).astype(BF)
    gatt_ref[...] = nt(ga, wo_ref[...]).astype(BF)
    part = tn(att_ref[...], ga)

    @pl.when(c == 0)
    def _():
        acc_ref[...] = part

    @pl.when(c != 0)
    def _():
        acc_ref[...] += part

    @pl.when(c == pl.num_programs(0) - 1)
    def _():
        dwo_ref[...] = acc_ref[...].astype(BF)


def mid_grad(heights, cot, mid, dn, gain, wo, att, slot):
    n, d = cot.shape
    rows = pl.BlockSpec((slot, d), lambda c, *_: (c, 0))
    whole = pl.BlockSpec((d, d), lambda c, *_: (0, 0))
    return pl.pallas_call(
        functools.partial(mid_grad_kernel, slot),
        grid_spec=pltpu.PrefetchScalarGridSpec(
            num_scalar_prefetch=1,
            grid=(n // slot,),
            in_specs=[rows, rows, rows, pl.BlockSpec((1, d), lambda c, *_: (0, 0)), whole, rows],
            out_specs=[rows, rows, whole],
            scratch_shapes=[pltpu.VMEM((d, d), F32)],
        ),
        out_shape=[
            jax.ShapeDtypeStruct((n, d), F32),
            jax.ShapeDtypeStruct((n, d), BF),
            jax.ShapeDtypeStruct((d, d), BF),
        ],
        compiler_params=params(),
        name="mid_grad",
    )(heights, cot, mid, dn, gain, wo, att)


def input_grad_kernel(gqkv_ref, w_ref, x_ref, gain_ref, gmid_ref, out_ref):
    gn = nt(gqkv_ref[...], w_ref[...])
    x = x_ref[...].astype(F32)
    inv = lax.rsqrt(jnp.mean(x * x, axis=-1, keepdims=True) + EPSILON)
    e = gn * gain_ref[...]
    out_ref[...] = (
        gmid_ref[...]
        + inv * e
        - x * (inv * inv * inv * jnp.mean(e * x, axis=-1, keepdims=True))
    )


def input_grad(gqkv, w, x, gain, gmid, rows):
    n, d = x.shape
    cols = w.shape[1]
    return pl.pallas_call(
        input_grad_kernel,
        grid=(n // rows,),
        in_specs=[
            pl.BlockSpec((rows, cols), lambda i: (i, 0)),
            pl.BlockSpec((d, cols), lambda i: (0, 0)),
            pl.BlockSpec((rows, d), lambda i: (i, 0)),
            pl.BlockSpec((1, d), lambda i: (0, 0)),
            pl.BlockSpec((rows, d), lambda i: (i, 0)),
        ],
        out_specs=pl.BlockSpec((rows, d), lambda i: (i, 0)),
        out_shape=jax.ShapeDtypeStruct((n, d), F32),
        compiler_params=params(),
        name="input_grad",
    )(gqkv, w, x, gain, gmid)


def angle_tables(positions):
    frequency = 1.0 / 10000.0 ** (jnp.arange(HEAD_DIM // 4, dtype=F32) * 4.0 / HEAD_DIM)
    frequency = jnp.tile(frequency, 8)
    first = (jnp.arange(HALF) // (HEAD_DIM // 4)) % 2 == 0
    crops, _, slot = positions.shape
    place = jnp.where(first, positions[:, 0, :, None], positions[:, 1, :, None])
    angles = (place.astype(F32) * frequency).reshape(crops * slot, HALF)
    return jnp.cos(angles), jnp.sin(angles)


def rot_order(w):
    rows, cols = w.shape
    w = w.reshape(rows, cols // GW, GROUP, 2, HEAD_DIM // 2)
    return w.transpose(0, 1, 3, 2, 4).reshape(rows, cols)


def natural_order(w):
    rows, cols = w.shape
    w = w.reshape(rows, cols // GW, 2, GROUP, HEAD_DIM // 2)
    return w.transpose(0, 1, 3, 2, 4).reshape(rows, cols)


def join_qkv(wq, wk, wv):
    rows, cols = wq.shape
    parts = [w.reshape(rows, cols // GW, GW) for w in (rot_order(wq), rot_order(wk), wv)]
    return jnp.concatenate(parts, axis=2).reshape(rows, 3 * cols)


def split_qkv(w):
    rows, cols = w.shape
    w = w.reshape(rows, cols // (3 * GW), 3, GW)
    q, k, v = (w[:, :, i].reshape(rows, cols // 3) for i in range(3))
    return natural_order(q), natural_order(k), v


def body(tokens, cotangent, crop_heights, rope_positions, gain_attn, w_query, w_key, w_value, w_out,
         gain_mlp, w_gate, w_up, w_down):
    crops = crop_heights.shape[0]
    rows, d = tokens.shape
    slot = rows // crops

    def gather(w):
        return lax.all_gather(w, "fsdp", axis=0, tiled=True)

    def reduce(g):
        local = lax.psum_scatter(g, "fsdp", scatter_dimension=0, tiled=True)
        return lax.psum(local, "rep").astype(F32)

    gains = lax.all_gather(jnp.stack([gain_attn, gain_mlp]), "fsdp", axis=1, tiled=True).astype(F32)
    gain1, gain2 = gains[:1], gains[1:]
    qkv_shard = join_qkv(w_query, w_key, w_value)
    wqkv = gather(qkv_shard)
    wo = gather(w_out)
    wg = gather(w_gate)
    wu = gather(w_up)
    wd = gather(w_down)
    cos, sin = angle_tables(rope_positions)
    nm1 = norm_call(tokens, gain1, slot)
    qkv, att, lse = attn_fwd(nm1, wqkv, cos, sin, slot)
    mid, nm2 = out_proj(crop_heights, tokens, att, wo, gain2, slot)
    out, dn, dwg, dwu, dwd = mlp(crop_heights, nm2, cotangent, mid, wg, wu, wd, slot)
    dwg, dwu, dwd = reduce(dwg), reduce(dwu), reduce(dwd)
    gmid, gatt, dwo = mid_grad(crop_heights, cotangent, mid, dn, gain2, wo, att, slot)
    dwo = reduce(dwo)
    gqkv, dwqkv = attn_bwd(qkv, gatt, att, lse, nm1, cos, sin, slot)
    dwqkv = reduce(dwqkv)
    grad_tokens = input_grad(gqkv, wqkv, tokens, gain1, gmid, slot)
    g1 = jnp.sum(dwqkv * qkv_shard.astype(F32), axis=1) / gain_attn.astype(F32)
    g2 = (
        jnp.sum(dwg * w_gate.astype(F32), axis=1) + jnp.sum(dwu * w_up.astype(F32), axis=1)
    ) / gain_mlp.astype(F32)
    dwq, dwk, dwv = split_qkv(dwqkv)
    return out, grad_tokens, g1, dwq, dwk, dwv, dwo, g2, dwg, dwu, dwd


def solution(mesh):
    in_specs = (
        P(("rep", "fsdp"), None),
        P(("rep", "fsdp"), None),
        P(("rep", "fsdp")),
        P(("rep", "fsdp"), None, None),
        P("fsdp"),
        P("fsdp", None),
        P("fsdp", None),
        P("fsdp", None),
        P("fsdp", None),
        P("fsdp"),
        P("fsdp", None),
        P("fsdp", None),
        P("fsdp", None),
    )
    out_specs = (
        P(("rep", "fsdp"), None),
        P(("rep", "fsdp"), None),
        P("fsdp"),
        P("fsdp", None),
        P("fsdp", None),
        P("fsdp", None),
        P("fsdp", None),
        P("fsdp"),
        P("fsdp", None),
        P("fsdp", None),
        P("fsdp", None),
    )
    return jax.shard_map(body, mesh=mesh, in_specs=in_specs, out_specs=out_specs, check_vma=False)
```

time: 1080 us -> 605 us (0.56); the launches traced: 1060 us -> 605 us
  matrix products: 461 us -> 0 us
  Pallas kernels: 0 us -> 286 us
  local copies, waits for them, and re-layouts: 174 us -> 11.1 us
  other arithmetic: 127 us -> 15.7 us
  blocking collectives: 43 us -> 13.5 us
  waiting for transfers between devices: 242 us -> 264 us
    dot_general x105 -> x0, matrix products: 461 us -> none  [the longest x7 90.1 us: through(): lax.dot_general(left, right, (((1,), (1,)), ((), ())), preferred_element_...]
    pallas_call x0 -> x7, Pallas kernels: none -> 286 us  [the longest x1 103 us: mlp(): pl.pallas_call(functools.partial(mlp_kernel, slot), grid_spec=pltpu.Prefe...]
    reduce_scatter x7 -> x5, waiting for transfers between devices: 232 us -> 119 us  [reduce(): local = lax.psum_scatter(g, 'fsdp', scatter_dimension=0, tiled=True)]
    all_gather x7 -> x5, waiting for transfers between devices: 0.05 us -> 89.5 us  [gather(): return lax.all_gather(w, 'fsdp', axis=0, tiled=True)]
    reshape x9 -> x3, local copies, waits for them, and re-layouts: 76.1 us -> 3.63 us  [the longest x1 1.56 us: split_qkv(): w = w.reshape(rows, cols // (3 * GW), 3, GW)]
    convert_element_type x33 -> x3, other arithmetic: 49.6 us -> 2.58 us  [the longest x2 2.57 us: reduce(): return lax.psum(local, 'rep').astype(F32)]
    psum x1, waiting for transfers between devices: 5.39 us -> 50.8 us  [reduce(): return lax.psum(local, 'rep').astype(F32)]
    convert_element_type x6 -> x1, local copies, waits for them, and re-layouts: 36.7 us -> 0.08 us  [body(): lax.all_gather(jnp.stack([gain_attn, gain_mlp]), 'fsdp', axis=1, tiled=True)]
  transfers between devices with their start and end apart: 15 -> 11, of which waited for: 5 -> 7; matrix products, arithmetic and copies ran while one was open for 39% -> 2% of each run, Pallas kernels for 0% -> 27%
where the time goes in v1:
time: 605 us
  Pallas kernels  286 us (47%)
  waiting for transfers between devices  264 us (44%)
  other arithmetic  15.7 us (3%)
  between operations  14.1 us (2%)
  blocking collectives  13.5 us (2%)
  local copies, waits for them, and re-layouts  11.1 us (2%)
    reduce_scatter x5, waiting for transfers between devices, reduce(): local = lax.psum_scatter(g, 'fsdp', scatter_dimension=0, tiled=True)  119 us
    pallas_call x1, Pallas kernels, mlp(): pl.pallas_call(functools.partial(mlp_kernel, slot), grid_spec=pltpu.Prefe...  103 us
    all_gather x5, waiting for transfers between devices, gather(): return lax.all_gather(w, 'fsdp', axis=0, tiled=True)  89.5 us
    pallas_call x1, Pallas kernels, attn_bwd(): pl.pallas_call(functools.partial(attn_bwd_kernel, slot, size), grid=(grou...  80.1 us
    pallas_call x1, Pallas kernels, attn_fwd(): pl.pallas_call(functools.partial(attn_fwd_kernel, slot, size), grid=(grou...  53.7 us
    psum x1, waiting for transfers between devices, reduce(): return lax.psum(local, 'rep').astype(F32)  50.8 us
    pallas_call x1, Pallas kernels, mid_grad(): pl.pallas_call(functools.partial(mid_grad_kernel, slot), grid_spec=pltpu....  17 us
    pallas_call x1, Pallas kernels, input_grad(): pl.pallas_call(input_grad_kernel, grid=(n // rows,), in_specs=[pl.BlockSp...  16.9 us
  transfers between devices with their start and end apart: 11, of which 7 were waited for; matrix products, arithmetic and copies ran while one was open for 2% of the time, Pallas kernels for 27%

profile of v1, /device:TPU:0, one launch (start us, length us, event | category | flops | bytes accessed | tf_op | source)
XLA Modules:
  0.0 605.0 jit_solution(4263601898959775533)
XLA Ops:
  7.3 1.1 copy.56
  8.4 1.1 copy.58
  9.5 1.1 copy.68
  10.5 0.1 pad_maximum_fusion
  10.7 1.0 copy.69
  11.7 0.7 all-gather.9.cloned.1.call-update
  12.5 0.7 all-gather.15.cloned.1.call-update
  13.2 0.5 all-gather.11.cloned.1.call-update
  13.8 0.5 all-gather.13.cloned.1.call-update
  14.4 0.1 mul.22
  14.5 13.5 %all-gather = bf16[8,96,2]{1,2,0:T(2,128)(2,1)S(1)} all-gather(bf16[1,96,2]{1,2,0:T(2,128)(2,1)S(1)} %maximum_bitcast_fusion), channel_id=1, replica_groups=mesh['rep'=4,'fsdp'=8] {'fsdp'}, dimensions={0}, use_global_device_ids=true | all-gather | bytes 3456 | tf_op jit(solution)/shard_map/all_gather | solution.py:527
  28.0 0.1 reshape.66
  28.1 0.1 slice_reduce_fusion.2
  28.2 0.1 broadcast_in_dim.25
  28.2 0.1 broadcast_in_dim.27
  28.3 0.6 fusion.4
  28.9 5.0 norm_in.1.nm_ref
  33.9 9.1 %fusion = (f32[2304,128]{1,0:T(8,128)}, f32[2304,128]{1,0:T(8,128)}) fusion(f32[128]{0:T(128)S(1)} %mul.22, s32[2304]{0:T(1024)S(1)} %broadcast_in_dim.27, s32[2304]{0:T(1024)S(1)} %broadcast_in_dim.25, pred[128]{0:T(512)(128)(4,1)S(1)} %fusion.2), kind=kLoop, calls=%fused_computation.1 | loop fusion | flops 884736 | bytes 2378368 | tf_op jit(solution)/shard_map/sin | solution.py:486
  43.0 13.1 %all-gather.7.cloned.1.call-done.w_ref = bf16[768,2304]{1,0:T(8,128)(2,1)} async-done(((bf16[96,2304]{1,0:T(8,128)(2,1)}), bf16[768,2304]{1,0:T(8,128)(2,1)}) %all-gather.7.cloned.1.call-update) | async-done | bytes 3538960 | tf_op jit(solution)/shard_map/all_gather | solution.py:521
  56.1 53.7 %attn_fwd.1 = (bf16[2304,2304]{1,0:T(8,128)(2,1)}, bf16[2304,768]{1,0:T(8,128)(2,1)}, f32[3,4,8,576]{3,2,1,0:T(8,128)}) custom-call(bf16[2304,768]{1,0:T(8,128)(2,1)} %norm_in.1.nm_ref, bf16[768,2304]{1,0:T(8,128)(2,1)} %all-gather.7.cloned.1.call-done.w_ref, f32[2304,128]{1,0:T(8,128)} %get-tuple-element.89.cos_ref, f32[2304,128]{1,0:T(8,128)} %get-tuple-element.88.sin_ref), custom_call_target="tpu_custom_call" | custom-call | tf_op jit(solution)/shard_map/attn_fwd/pallas_call | solution.py:122
  109.8 10.0 %out_proj.1 = (f32[2304,768]{1,0:T(8,128)}, bf16[2304,768]{1,0:T(8,128)(2,1)}) custom-call(s32[4]{0:T(128)} %heights_ref.5, bf16[2304,768]{1,0:T(8,128)(2,1)} %x_ref.5, bf16[2304,768]{1,0:T(8,128)(2,1)} %get-tuple-element.26.att_ref, bf16[768,768]{1,0:T(8,128)(2,1)} %all-gather.9.cloned.1.call-done.wo_ref, f32[1,768]{1,0:T(1,128)} %get-tuple-element.90.gain_ref), custom_call_target="tpu_custom_call" | custom-call | tf_op jit(solution)/shard_map/out_proj/pallas_call | solution.py:269
  119.8 37.8 %all-gather.11.cloned.1.call-done.wg_ref = bf16[768,2048]{1,0:T(8,128)(2,1)} async-done(((bf16[96,2048]{1,0:T(8,128)(2,1)}), bf16[768,2048]{1,0:T(8,128)(2,1)}) %all-gather.11.cloned.1.call-update) | async-done | bytes 3145744 | tf_op jit(solution)/shard_map/all_gather | solution.py:521
  157.6 38.7 %all-gather.13.cloned.1.call-done.wu_ref = bf16[768,2048]{1,0:T(8,128)(2,1)} async-done(((bf16[96,2048]{1,0:T(8,128)(2,1)}), bf16[768,2048]{1,0:T(8,128)(2,1)}) %all-gather.13.cloned.1.call-update) | async-done | bytes 3145744 | tf_op jit(solution)/shard_map/all_gather | solution.py:521
  196.2 103.2 %mlp.1 = (bf16[2304,768]{1,0:T(8,128)(2,1)}, f32[2304,768]{1,0:T(8,128)}, bf16[768,2048]{1,0:T(8,128)(2,1)}, bf16[768,2048]{1,0:T(8,128)(2,1)}, bf16[2048,768]{1,0:T(8,128)(2,1)}) custom-call(s32[4]{0:T(128)} %heights_ref.5, bf16[2304,768]{1,0:T(8,128)(2,1)} %get-tuple-element.27.nm_ref, bf16[2304,768]{1,0:T(8,128)(2,1)} %cot_ref.3, ...), custom_call_target="tpu_custom_call" | custom-call | tf_op jit(solution)/shard_map/mlp/pallas_call | solution.py:365
  299.5 17.0 %mid_grad.1 = (f32[2304,768]{1,0:T(8,128)}, bf16[2304,768]{1,0:T(8,128)(2,1)}, bf16[768,768]{1,0:T(8,128)(2,1)}) custom-call(s32[4]{0:T(128)} %heights_ref.5, bf16[2304,768]{1,0:T(8,128)(2,1)} %cot_ref.3, f32[2304,768]{1,0:T(8,128)} %get-tuple-element.28.mid_ref, f32[2304,768]{1,0:T(8,128)} %get-tuple-element.31.dn_ref, ...), custom_call_target="tpu_custom_call" | custom-call | tf_op jit(solution)/shard_map/mid_grad/pallas_call | solution.py:428
  316.5 0.7 reduce-scatter.10.cloned.1.call-update
  317.2 0.7 reduce-scatter.12.cloned.1.call-update
  318.0 0.7 reduce-scatter.14.cloned.1.call-update
  318.7 80.1 %attn_bwd.1 = (bf16[2304,2304]{1,0:T(8,128)(2,1)}, bf16[768,2304]{1,0:T(8,128)(2,1)}) custom-call(bf16[2304,2304]{1,0:T(8,128)(2,1)} %get-tuple-element.30.qkv_ref, bf16[2304,768]{1,0:T(8,128)(2,1)} %get-tuple-element.32.go_ref, bf16[2304,768]{1,0:T(8,128)(2,1)} %get-tuple-element.26.att_ref, f32[3,4,8,576]{3,2,1,0:T(8,128)} %get-tuple-element.33.lse_ref, ...), custom_call_target="tpu_custom_call" | custom-call | tf_op jit(solution)/shard_map/attn_bwd/pallas_call | solution.py:226
  398.9 0.0 all-reduce.3.cloned.1.call-start
  399.0 32.0 %reduce-scatter.12.cloned.1.call-done = bf16[96,2048]{1,0:T(8,128)(2,1)} async-done(((bf16[768,2048]{1,0:T(8,128)(2,1)}), bf16[96,2048]{1,0:T(8,128)(2,1)}) %reduce-scatter.12.cloned.1.call-update) | async-done | bytes 393232 | tf_op jit(solution)/shard_map/reduce_scatter | solution.py:524
  431.0 41.8 %reduce-scatter.14.cloned.1.call-done = bf16[256,768]{1,0:T(8,128)(2,1)} async-done(((bf16[2048,768]{1,0:T(8,128)(2,1)}), bf16[256,768]{1,0:T(8,128)(2,1)}) %reduce-scatter.14.cloned.1.call-update) | async-done | bytes 393232 | tf_op jit(solution)/shard_map/reduce_scatter | solution.py:524
  472.7 45.7 %reduce-scatter.6.cloned.1.call-done = bf16[96,2304]{1,0:T(8,128)(2,1)} async-done(((bf16[768,2304]{1,0:T(8,128)(2,1)}), bf16[96,2304]{1,0:T(8,128)(2,1)}) %reduce-scatter.6.cloned.1.call-update) | async-done | bytes 442384 | tf_op jit(solution)/shard_map/reduce_scatter | solution.py:524
  518.4 16.9 %input_grad.1 = f32[2304,768]{1,0:T(8,128)} custom-call(bf16[2304,2304]{1,0:T(8,128)(2,1)} %get-tuple-element.34.gqkv_ref, bf16[768,2304]{1,0:T(8,128)(2,1)} %all-gather.7.cloned.1.call-done.w_ref, bf16[2304,768]{1,0:T(8,128)(2,1)} %x_ref.5, f32[1,768]{1,0:T(1,128)} %get-tuple-element.91.gain_ref, f32[2304,768]{1,0:T(8,128)} %get-tuple-element.35.gmid_ref), custom_call_target="tpu_custom_call" | custom-call | tf_op jit(solution)/shard_map/input_grad/pallas_call | solution.py:462
  535.3 50.8 %all-reduce.3.cloned.1.call-done = (bf16[96,2304]{1,0:T(8,128)(2,1)}, bf16[96,768]{1,0:T(8,128)(2,1)}, bf16[96,2048]{1,0:T(8,128)(2,1)}, bf16[96,2048]{1,0:T(8,128)(2,1)}, bf16[256,768]{1,0:T(8,128)(2,1)}) async-done(((bf16[96,2304]{1,0:T(8,128)(2,1)}, bf16[96,768]{1,0:T(8,128)(2,1)}, bf16[96,2048]{1,0:T(8,128)(2,1)}, bf16[96,2048]{1,0:T(8,128)(2,1)}, bf16[256,768]{1,0:T(8,128)(2,1)}), ...) | async-done | bytes 1769488 | tf_op jit(solution)/shard_map/psum | solution.py:525
  586.2 1.3 multiply_reduce_fusion
  587.5 1.6 reshape.61
  589.0 0.5 convert_divide_fusion.1
  589.6 1.6 convert_element_type.42
  591.2 0.9 convert_element_type.48
  592.2 1.3 slice_reduce_fusion
  593.4 0.8 copy.70
  594.2 0.2 copy.64
  594.4 0.9 copy.67
  595.3 0.2 copy.62
  595.5 0.9 copy.66
  596.4 1.5 multiply_reduce_fusion.1
  597.9 0.5 convert_divide_fusion
  (45 shorter events, 0.7 us)
Async XLA Ops:
  7.2 7.3 %copy-start.8 = (bf16[96]{0:T(256)(128)(2,1)S(1)}, bf16[96]{0:T(256)(128)(2,1)}, u32[]{:S(2)}) copy-start(bf16[96]{0:T(256)(128)(2,1)} %param.17) | copy-start | bytes 580
  7.2 7.3 %copy-start.7 = (bf16[96]{0:T(256)(128)(2,1)S(1)}, bf16[96]{0:T(256)(128)(2,1)}, u32[]{:S(2)}) copy-start(bf16[96]{0:T(256)(128)(2,1)} %param.22) | copy-start | bytes 580
  7.2 20.9 %copy-start.6 = (s32[4,2,576]{2,1,0:T(2,128)S(1)}, s32[4,2,576]{2,1,0:T(2,128)}, u32[]{:S(2)}) copy-start(s32[4,2,576]{2,1,0:T(2,128)} %param.16) | copy-start | bytes 55300
  7.2 48.9 %all-gather.7.cloned.1.call-start = ((), (), s32[]{:S(2)}) async-start(), calls=%async_computation.5 | async-start | bytes 3981312 | tf_op jit(solution)/shard_map/all_gather | solution.py:521
  11.7 98.1 %all-gather.9.cloned.1.call-start = ((), (), s32[]{:S(2)}) async-start(), calls=%async_computation.6 | async-start | bytes 1327104 | tf_op jit(solution)/shard_map/all_gather | solution.py:521
  12.4 107.3 %all-gather.15.cloned.1.call-start = ((), (), s32[]{:S(2)}) async-start(), calls=%async_computation.9 | async-start | bytes 3538944 | tf_op jit(solution)/shard_map/all_gather | solution.py:521
  13.2 144.4 %all-gather.11.cloned.1.call-start = ((), (), s32[]{:S(2)}) async-start(), calls=%async_computation.7 | async-start | bytes 3538944 | tf_op jit(solution)/shard_map/all_gather | solution.py:521
  13.8 182.5 %all-gather.13.cloned.1.call-start = ((), (), s32[]{:S(2)}) async-start(), calls=%async_computation.8 | async-start | bytes 3538944 | tf_op jit(solution)/shard_map/all_gather | solution.py:521
  14.3 384.6 %reduce-scatter.8.cloned.1.call-start = ((), (), s32[]{:S(2)}) async-start(), calls=%async_computation.11 | async-start | bytes 1327104 | tf_op jit(solution)/shard_map/reduce_scatter | solution.py:524
  316.5 82.5 %reduce-scatter.10.cloned.1.call-start = ((), (), s32[]{:S(2)}) async-start(), calls=%async_computation.12 | async-start | bytes 3538944 | tf_op jit(solution)/shard_map/reduce_scatter | solution.py:524
  317.2 113.8 %reduce-scatter.12.cloned.1.call-start = ((), (), s32[]{:S(2)}) async-start(), calls=%async_computation.13 | async-start | bytes 3538944 | tf_op jit(solution)/shard_map/reduce_scatter | solution.py:524
  318.0 154.8 %reduce-scatter.14.cloned.1.call-start = ((), (), s32[]{:S(2)}) async-start(), calls=%async_computation.14 | async-start | bytes 3538944 | tf_op jit(solution)/shard_map/reduce_scatter | solution.py:524
  318.7 199.7 %reduce-scatter.6.cloned.1.call-start = ((), (), s32[]{:S(2)}) async-start(), calls=%async_computation.10 | async-start | bytes 3981312 | tf_op jit(solution)/shard_map/reduce_scatter | solution.py:524
  398.9 187.3 %all-reduce.3.cloned.1.call-start = ((), (), s32[]{:S(2)}) async-start(), calls=%async_computation.15 | async-start | bytes 3538944 | tf_op jit(solution)/shard_map/psum | solution.py:525
  518.4 67.8 %copy-start = (bf16[96,2304]{1,0:T(8,128)(2,1)S(1)}, bf16[96,2304]{1,0:T(8,128)(2,1)}, u32[]{:S(2)}) copy-start(bf16[96,2304]{1,0:T(8,128)(2,1)} %copy.69) | copy-start | bytes 1327108
  586.2 5.0 copy-start.3
  592.1 4.3 copy-start.1
  592.1 4.3 copy-start.2
  592.1 4.3 copy-start.4
  592.1 4.3 copy-start.5
Sparse Core Ops, SparseCore 0:
  11.8 44.2 all-gather.6
  57.7 21.5 all-gather.8
  81.0 37.8 all-gather.14
  120.4 37.1 all-gather.10
  159.1 37.1 all-gather.12
  316.6 31.7 reduce-scatter.7
  350.6 38.3 reduce-scatter.9
  391.4 39.5 reduce-scatter.11
  433.3 39.4 reduce-scatter.13
  475.5 42.8 reduce-scatter.5
  522.5 63.6 all-reduce.2

commit v2 on v1

v2 whole, which is shorter than its diff:
```python
import functools
import jax
import jax.numpy as jnp
import numpy as np
from jax import lax
from jax.experimental import pallas as pl
from jax.experimental.pallas import tpu as pltpu
from jax.sharding import PartitionSpec as P

HEAD_DIM = 64
COLS = 24
EPSILON = 1e-05
GROUP = 4
GW = GROUP * HEAD_DIM
HALF = GW // 2
BF = jnp.bfloat16
F32 = jnp.float32


def nn(a, b):
    return lax.dot_general(a, b, (((1,), (0,)), ((), ())), preferred_element_type=F32)


def nt(a, b):
    return lax.dot_general(a, b, (((1,), (1,)), ((), ())), preferred_element_type=F32)


def tn(a, b):
    return lax.dot_general(a, b, (((0,), (0,)), ((), ())), preferred_element_type=F32)


def params(limit=60):
    return pltpu.CompilerParams(vmem_limit_bytes=limit * 1024 * 1024)


def cost(flops, moved):
    return pl.CostEstimate(flops=int(flops), transcendentals=0, bytes_accessed=int(moved))


def inverse_rms(x):
    return lax.rsqrt(jnp.mean(x * x, axis=-1, keepdims=True) + EPSILON)


def norm_kernel(x_ref, out_ref):
    x = x_ref[...].astype(F32)
    out_ref[...] = (x * inverse_rms(x)).astype(BF)


def norm_call(x, rows):
    n, d = x.shape
    spec = pl.BlockSpec((rows, d), lambda i: (i, 0))
    return pl.pallas_call(
        norm_kernel,
        grid=(n // rows,),
        in_specs=[spec],
        out_specs=spec,
        out_shape=jax.ShapeDtypeStruct((n, d), BF),
        compiler_params=params(),
        cost_estimate=cost(0, 4 * n * d),
        name="norm_in",
    )(x)


def head_masks():
    lane = lax.broadcasted_iota(jnp.int32, (1, GW), 1)
    rot = [((lane % HALF) // (HEAD_DIM // 2) == h) for h in range(GROUP)]
    nat = [(lane // HEAD_DIM == h) for h in range(GROUP)]
    return rot, nat


def mask_to(x, m):
    return x * jnp.where(m, 1.0, 0.0).astype(x.dtype)


def blocks_of(total, size):
    return [(s, min(s + size, total)) for s in range(0, total, size)]


def attn_fwd_kernel(slot, size, ids_ref, nm_ref, cos_ref, sin_ref, own_hbm, oth_hbm,
                    qkv_ref, att_ref, lse_ref, w_out_ref, sem):
    group = pl.program_id(0)
    crop = pl.program_id(1)
    crops = pl.num_programs(1)
    zs = own_hbm.shape[1]
    rep, z, core = ids_ref[crops], ids_ref[crops + 1], ids_ref[crops + 2]

    @pl.when(crop == 0)
    def _():
        made = []
        for hbm, place in ((own_hbm, core), (oth_hbm, 1 - core)):
            for kind in range(4):
                for j in range(zs):
                    src = hbm.at[kind ^ rep, j, :, pl.ds(pl.multiple_of(group * GW, GW), GW)]
                    dst = w_out_ref.at[(z + j) & (zs - 1), place, :, pl.ds(kind * GW, GW)]
                    made.append(pltpu.make_async_copy(src, dst, sem.at[len(made)]))
        for copy in made:
            copy.start()
        for copy in made:
            copy.wait()

    nm = nm_ref[...]
    cos = cos_ref[...]
    sin = sin_ref[...]
    rot_m, nat_m = head_masks()
    d = nm.shape[1]

    def rotated(lo, scale):
        u = nn(nm, w_out_ref[:, :, :, lo : lo + GW].reshape(d, GW))
        a, b = u[:, :HALF], u[:, HALF:]
        r = jnp.concatenate([a * cos - b * sin, a * sin + b * cos], axis=1)
        return r.astype(BF) * jnp.asarray(scale, BF)

    q = rotated(0, HEAD_DIM ** (-0.5))
    k = rotated(GW, 1.0)
    v = nn(nm, w_out_ref[:, :, :, 2 * GW : 3 * GW].reshape(d, GW)).astype(BF)
    qkv_ref[:, :GW] = q
    qkv_ref[:, GW : 2 * GW] = k
    qkv_ref[:, 2 * GW :] = v
    qs = [mask_to(q, m) for m in rot_m]
    vs = [mask_to(v, m) for m in nat_m]
    lane = lax.broadcasted_iota(jnp.int32, (1, 128), 1)
    units = [(s, e, h) for s, e in blocks_of(slot, size) for h in range(GROUP)]

    def scores(s, e, h):
        qh = qs[h][s:e]
        return nt(qh, k[s:e]), nt(qh, k[:s]) if s else None

    out = logs = None
    ready = scores(*units[0])
    for i, (s, e, h) in enumerate(units):
        later = scores(*units[i + 1]) if i + 1 < len(units) else None
        diag, left = ready
        row = lax.broadcasted_iota(jnp.int32, (e - s, e - s), 0)
        col = lax.broadcasted_iota(jnp.int32, (e - s, e - s), 1)
        diag = jnp.where(row >= col, diag, -1e30)
        top = jnp.max(diag, axis=-1, keepdims=True)
        if s:
            top = jnp.maximum(top, jnp.max(left, axis=-1, keepdims=True))
        pd = jnp.exp(diag - top)
        total = jnp.sum(pd, axis=-1, keepdims=True)
        o = nn(pd.astype(BF), vs[h][s:e])
        if s:
            pleft = jnp.exp(left - top)
            total = total + jnp.sum(pleft, axis=-1, keepdims=True)
            o = o + nn(pleft.astype(BF), vs[h][:s])
        o = o * (1.0 / total)
        out = out + o if h else o
        logs = jnp.where(lane == h, top + jnp.log(total), logs if h else 0.0)
        if h == GROUP - 1:
            att_ref[s:e, :] = out.astype(BF)
            lse_ref[0, 0, :, s:e] = logs.T[:8]
        ready = later


def attn_fwd(ids, nm, cos, sin, own, oth, slot, size=256):
    n, d = nm.shape
    crops = n // slot
    kinds, zs, rows, width = own.shape
    groups = width // GW
    hbm = pl.BlockSpec(memory_space=pl.ANY)
    crop_spec = lambda w: pl.BlockSpec((slot, w), lambda g, c, *_: (c, 0))
    qkv, att, lse, w = pl.pallas_call(
        functools.partial(attn_fwd_kernel, slot, size),
        grid_spec=pltpu.PrefetchScalarGridSpec(
            num_scalar_prefetch=1,
            grid=(groups, crops),
            in_specs=[crop_spec(d), crop_spec(HALF), crop_spec(HALF), hbm, hbm],
            out_specs=[
                pl.BlockSpec((slot, 3 * GW), lambda g, c, *_: (c, g)),
                pl.BlockSpec((slot, GW), lambda g, c, *_: (c, g)),
                pl.BlockSpec((1, 1, 8, slot), lambda g, c, *_: (g, c, 0, 0)),
                pl.BlockSpec((zs, 2, rows, 4 * GW), lambda g, c, *_: (0, 0, 0, g)),
            ],
            scratch_shapes=[pltpu.SemaphoreType.DMA((8 * zs,))],
        ),
        out_shape=[
            jax.ShapeDtypeStruct((n, groups * 3 * GW), BF),
            jax.ShapeDtypeStruct((n, groups * GW), BF),
            jax.ShapeDtypeStruct((groups, crops, 8, slot), F32),
            jax.ShapeDtypeStruct((zs, 2, rows, groups * 4 * GW), BF),
        ],
        compiler_params=params(),
        cost_estimate=cost(8e6 * groups * n, 2 * n * d),
        name="attn_fwd",
    )(ids, nm, cos, sin, own, oth)
    return qkv, att, lse, w.reshape(d, groups * 4 * GW)


def attn_bwd_kernel(slot, size, qkv_ref, go_ref, att_ref, lse_ref, nm_ref, cos_ref, sin_ref, *refs):
    gqkv_ref, dw_ref, dst_ref, dq_ref, acc_ref = refs[-5:]
    crop = pl.program_id(1)
    q = qkv_ref[:, :GW]
    k = qkv_ref[:, GW : 2 * GW]
    v = qkv_ref[:, 2 * GW :]
    go = go_ref[...]
    rot_m, nat_m = head_masks()
    prod = go.astype(F32) * att_ref[...].astype(F32)
    hi = prod.astype(BF)
    lo = (prod - hi.astype(F32)).astype(BF)
    pick = (
        lax.broadcasted_iota(jnp.int32, (8, GW), 1) // HEAD_DIM
        == lax.broadcasted_iota(jnp.int32, (8, GW), 0)
    )
    pick = jnp.where(pick, 1.0, 0.0).astype(BF)
    delta = nt(pick, hi) + nt(pick, lo)
    blocks = blocks_of(slot, size)
    dk = [None] * len(blocks)
    dv = [None] * len(blocks)
    qms = [mask_to(q, m) for m in rot_m]
    kms = [mask_to(k, m) for m in rot_m]
    gms = [mask_to(go, m) for m in nat_m]
    units = []
    for h in range(GROUP):
        for j, (s, e) in enumerate(blocks):
            units.append((h, j, s, e, s, e))
            if e < slot:
                units.append((h, j, s, e, e, slot))

    def scores(h, j, s, e, ps, pe):
        return nt(k[s:e], qms[h][ps:pe]), nt(v[s:e], gms[h][ps:pe])

    ready = scores(*units[0])
    for i, (h, j, s, e, ps, pe) in enumerate(units):
        later = scores(*units[i + 1]) if i + 1 < len(units) else None
        sc, dp = ready
        p = jnp.exp(sc - lse_ref[0, 0, h : h + 1, ps:pe])
        if ps == s:
            row = lax.broadcasted_iota(jnp.int32, (e - s, e - s), 0)
            col = lax.broadcasted_iota(jnp.int32, (e - s, e - s), 1)
            p = jnp.where(col >= row, p, 0.0)
        ds = (p * (dp - delta[h : h + 1, ps:pe])).astype(BF)
        dst_ref[h, s:e, ps:pe] = ds
        dvp = nn(p.astype(BF), gms[h][ps:pe])
        dkp = nn(ds, qms[h][ps:pe])
        dv[j] = dvp if dv[j] is None else dv[j] + dvp
        dk[j] = dkp if dk[j] is None else dk[j] + dkp
        if i + 1 == len(units) or units[i + 1][0] != h:
            for bs, be in blocks:
                part = tn(dst_ref[h, :be, bs:be], kms[h][:be])
                if h:
                    dq_ref[bs:be] += part
                else:
                    dq_ref[bs:be] = part
        ready = later
    cos = cos_ref[...]
    sin = sin_ref[...]

    def back(u, c, t):
        a, b = u[:, :HALF], u[:, HALF:]
        return jnp.concatenate([a * c + b * t, b * c - a * t], axis=1).astype(BF)

    for j, (s, e) in enumerate(blocks):
        c, t = cos[s:e], sin[s:e]
        gqkv_ref[s:e, :GW] = back(dq_ref[s:e] * (HEAD_DIM ** (-0.5)), c, t)
        gqkv_ref[s:e, GW : 2 * GW] = back(dk[j], c, t)
        gqkv_ref[s:e, 2 * GW :] = dv[j].astype(BF)
    part = tn(nm_ref[...], gqkv_ref[...])

    @pl.when(crop == 0)
    def _():
        acc_ref[...] = part

    @pl.when(crop != 0)
    def _():
        acc_ref[...] += part

    @pl.when(crop == pl.num_programs(1) - 1)
    def _():
        dw_ref[...] = acc_ref[...].astype(BF)


def attn_bwd(qkv, go, att, lse, nm, cos, sin, slot, place, first, joint=None, size=256):
    n, d = nm.shape
    crops = n // slot
    more = [] if joint is None else [joint]
    column = 0 if joint is None else first + place + 1
    row_spec = lambda w, at: pl.BlockSpec((slot, w), lambda g, c: (c, at))
    crop_spec = lambda w: pl.BlockSpec((slot, w), lambda g, c: (c, 0))
    return pl.pallas_call(
        functools.partial(attn_bwd_kernel, slot, size),
        grid=(1, crops),
        in_specs=[
            row_spec(3 * GW, place),
            row_spec(GW, first + place),
            row_spec(GW, place),
            pl.BlockSpec((1, 1, 8, slot), lambda g, c: (place, c, 0, 0)),
            crop_spec(d),
            crop_spec(HALF),
            crop_spec(HALF),
        ]
        + [pl.BlockSpec(memory_space=pl.ANY)] * len(more),
        out_specs=[crop_spec(3 * GW), pl.BlockSpec((d, 3 * GW), lambda g, c: (0, column))],
        out_shape=[
            jax.ShapeDtypeStruct((n, 3 * GW), BF),
            jax.ShapeDtypeStruct((d, 3 * GW) if joint is None else joint.shape, BF),
        ],
        input_output_aliases={7: 1} if more else {},
        scratch_shapes=[
            pltpu.VMEM((GROUP, slot, slot), BF),
            pltpu.VMEM((slot, GW), F32),
            pltpu.VMEM((d, 3 * GW), F32),
        ],
        compiler_params=params(),
        cost_estimate=cost(12e6 * n, 2 * n * d),
        name="attn_bwd",
    )(qkv, go, att, lse, nm, cos, sin, *more)


def valid_rows(ids_ref, tile, rows, slot):
    row = tile * rows + lax.broadcasted_iota(jnp.int32, (rows, 1), 0)
    crop = row // slot
    first = tile * rows // slot
    limit = jnp.zeros((rows, 1), jnp.int32)
    for i in range(-(-rows // slot) + 1):
        index = first + i
        limit = jnp.where(crop == index, ids_ref[index] * COLS, limit)
    return row - crop * slot < limit


def out_weights(weights, d):
    arrays, specs = [], []
    for w in weights:
        for g in range(w.shape[1] // (4 * GW)):
            arrays.append(w)
            specs.append(pl.BlockSpec((d, GW), lambda c, *_, g=g: (0, 4 * g + 3)))
    return arrays, specs


def out_proj_kernel(slot, n_att, ids_ref, x_ref, *refs):
    att_refs, refs = refs[:n_att], refs[n_att:]
    *wo_refs, mid_ref, nm_ref = refs
    valid = valid_rows(ids_ref, pl.program_id(0), x_ref.shape[0], slot)
    att = jnp.concatenate([a[...] for a in att_refs], axis=1)
    proj = jnp.concatenate([nn(att, w[...]) for w in wo_refs], axis=1)
    mid = x_ref[...].astype(F32) + jnp.where(valid, proj, 0.0)
    mid_ref[...] = mid
    nm_ref[...] = (mid * inverse_rms(mid)).astype(BF)


def out_proj(ids, x, atts, weights, slot, tile):
    n, d = x.shape
    rows = lambda w: pl.BlockSpec((tile, w), lambda c, *_: (c, 0))
    wos, wo_specs = out_weights(weights, d)
    return pl.pallas_call(
        functools.partial(out_proj_kernel, slot, len(atts)),
        grid_spec=pltpu.PrefetchScalarGridSpec(
            num_scalar_prefetch=1,
            grid=(n // tile,),
            in_specs=[rows(d)] + [rows(a.shape[1]) for a in atts] + wo_specs,
            out_specs=[rows(d), rows(d)],
        ),
        out_shape=[jax.ShapeDtypeStruct((n, d), F32), jax.ShapeDtypeStruct((n, d), BF)],
        compiler_params=params(),
        cost_estimate=cost(2 * n * d * d, 10 * n * d),
        name="out_proj",
    )(ids, x, *atts, *wos)


PACK = 512
TILE = 768
SHARDS = 8


def halves(w, axis):
    shape = w.shape[:axis] + (-1, 2, w.shape[axis] // (2 * SHARDS) if axis else w.shape[0] // 2) + w.shape[axis + 1 :]
    w = w.reshape(shape)
    return [
        lax.index_in_dim(w, i, axis + 1, keepdims=False).reshape(w.shape[:axis] + (-1,) + w.shape[axis + 3 :])
        for i in range(2)
    ]


def pack_mlp(gate, up, down):
    wide = [w[:, i : i + PACK] for w in (gate, up) for i in range(0, w.shape[1], PACK)]
    half = down.shape[0] // 2
    tail = down[:, PACK:]
    fold = jnp.concatenate([tail[:half], tail[half:]], axis=1)
    return jnp.concatenate(wide + [down[:, :PACK], fold], axis=0)


def unpack_mlp(pack, rows, d):
    chunks = 2
    gate, up = (
        jnp.concatenate([pack[i * rows : (i + 1) * rows] for i in range(s, s + chunks)], axis=1)
        for s in (0, chunks)
    )
    base = 2 * chunks * rows
    deep = (pack.shape[0] - base) * PACK // d
    fold = pack[base + deep :]
    tail = jnp.concatenate([fold[:, : d - PACK], fold[:, d - PACK :]], axis=0)
    return gate, up, jnp.concatenate([pack[base : base + deep], tail], axis=1)


def mlp_kernel(slot, final, step, ids_ref, nm_ref, cot_ref, part_ref, *refs):
    if final:
        before_ref, *refs = refs
    (pack_hbm, out_ref, dn_ref, grad_hbm, wg_buf, wu_buf, wd_buf, hid_ref, gg_ref, gu_ref,
     ag_ref, au_ref, ad_ref, sg_ref, su_ref, sd_ref, in_sem, out_sem) = refs
    tile = pl.program_id(0)
    d = nm_ref.shape[1]
    chunks, shards, rows, _ = sg_ref.shape
    units = chunks * PACK
    some = shards // chunks
    deep = sd_ref.shape[1]
    base = 2 * chunks * rows
    side = d - PACK

    def pieces(hbm, wg, wu, wd):
        for i in range(chunks):
            yield hbm.at[:, pl.ds(i * rows, rows), :], wg.at[i]
            yield hbm.at[:, pl.ds((chunks + i) * rows, rows), :], wu.at[i]
        yield hbm.at[:, pl.ds(base, deep), :], wd.at[:, :, pl.ds(0, PACK)]
        for i in range(2):
            yield (
                hbm.at[:, pl.ds(base + deep, deep // 2), pl.ds(i * side, side)],
                wd.at[:, pl.ds(i * (deep // 2), deep // 2), pl.ds(PACK, side)],
            )

    @pl.when(tile == 0)
    def _():
        made = pieces(pack_hbm, wg_buf, wu_buf, wd_buf)
        made = [pltpu.make_async_copy(a, b, in_sem.at[i]) for i, (a, b) in enumerate(made)]
        for copy in made:
            copy.start()
        ag_ref[...] = jnp.zeros_like(ag_ref)
        au_ref[...] = jnp.zeros_like(au_ref)
        ad_ref[...] = jnp.zeros_like(ad_ref)
        for copy in made:
            copy.wait()

    valid = valid_rows(ids_ref, tile, nm_ref.shape[0], slot)
    nm = nm_ref[...]
    gb = jnp.where(valid, cot_ref[...], jnp.zeros((), BF))
    wd = wd_buf[...].reshape(units, d)

    def wide(buf, i):
        at = i * step
        return buf[at // PACK, :, :, at % PACK : at % PACK + step].reshape(d, step)

    def first(i):
        return (
            nn(nm, wide(wg_buf, i)),
            nn(nm, wide(wu_buf, i)),
            nt(gb, wd[i * step : (i + 1) * step]),
        )

    def second(i, g, u, gh):
        cols = slice(i * step, (i + 1) * step)
        sg = 0.5 * jnp.tanh(0.5 * g) + 0.5
        act = g * sg
        hid_ref[:, cols] = (act * u).astype(BF)
        gu_ref[:, cols] = (gh * act).astype(BF)
        gg_ref[:, cols] = (gh * u * (sg + act * (1.0 - sg))).astype(BF)

    ready = first(0)
    for i in range(1, units // step):
        later = first(i)
        second(i - 1, *ready)
        ready = later
    second(units // step - 1, *ready)
    nmt = nm.T
    gbt = gb.T
    o = part_ref[...] + jnp.where(valid, nn(hid_ref[...], wd), 0.0)
    out_ref[...] = o.astype(out_ref.dtype)
    dn = before_ref[...] if final else 0.0
    for i in range(chunks):
        cols = slice(i * PACK, (i + 1) * PACK)
        dn = dn + nt(gg_ref[:, cols], wg_buf[i].reshape(d, PACK)) + nt(gu_ref[:, cols], wu_buf[i].reshape(d, PACK))
    dn_ref[...] = dn
    for i in range(chunks):
        cols = slice(i * PACK, (i + 1) * PACK)
        ag_ref[i] += nn(nmt, gg_ref[:, cols])
        au_ref[i] += nn(nmt, gu_ref[:, cols])
        ad_ref[i] += nn(gbt, hid_ref[:, cols])

    @pl.when(tile == pl.num_programs(0) - 1)
    def _():
        sg_ref[...] = ag_ref[...].astype(BF).reshape(sg_ref.shape)
        su_ref[...] = au_ref[...].astype(BF).reshape(su_ref.shape)
        for i in range(chunks):
            sd_ref[i * some : (i + 1) * some] = ad_ref[i].astype(BF).T.reshape(some, deep, d)
        made = pieces(grad_hbm, sg_ref, su_ref, sd_ref)
        made = [pltpu.make_async_copy(b, a, out_sem.at[i]) for i, (a, b) in enumerate(made)]
        for copy in made:
            copy.start()
        for copy in made:
            copy.wait()


def mlp(ids, nm, cot, part, before, pack, slot, tile, step=256):
    n, d = nm.shape
    rows = d // SHARDS
    chunks = 2
    deep = chunks * PACK // SHARDS
    final = before is not None
    spec = pl.BlockSpec((tile, d), lambda i, *_: (i, 0))
    hbm = pl.BlockSpec(memory_space=pl.ANY)
    packed = pltpu.VMEM((chunks, SHARDS, rows, PACK), BF)
    units = pltpu.VMEM((tile, chunks * PACK), BF)
    sums = pltpu.VMEM((chunks, d, PACK), F32)
    return pl.pallas_call(
        functools.partial(mlp_kernel, slot, final, step),
        grid_spec=pltpu.PrefetchScalarGridSpec(
            num_scalar_prefetch=1,
            grid=(n // tile,),
            in_specs=[spec] * (3 + final) + [hbm],
            out_specs=[spec, spec, hbm],
            scratch_shapes=[packed, packed, pltpu.VMEM((SHARDS, deep, d), BF)]
            + [units] * 3
            + [sums] * 3
            + [packed, packed, pltpu.VMEM((SHARDS, deep, d), BF)]
            + [pltpu.SemaphoreType.DMA((2 * chunks + 3,))] * 2,
        ),
        out_shape=[
            jax.ShapeDtypeStruct((n, d), BF if final else F32),
            jax.ShapeDtypeStruct((n, d), F32),
            jax.ShapeDtypeStruct(pack.shape, BF),
        ],
        compiler_params=params(),
        cost_estimate=cost(24e6 * n, 20 * n * d),
        name="mlp",
    )(ids, nm, cot, part, *([before] if final else []), pack)


def norm_back(scaled, field):
    inv = inverse_rms(field)
    return inv * scaled - field * (inv * inv * inv * jnp.mean(scaled * field, axis=-1, keepdims=True))


def mid_grad_kernel(slot, n_att, ids_ref, cot_ref, mid_ref, dn_ref, *refs):
    att_refs, refs = refs[:n_att], refs[n_att:]
    *wo_refs, gmid_ref, gatt_ref, dwo_ref, acc_ref = refs
    c = pl.program_id(0)
    valid = valid_rows(ids_ref, c, cot_ref.shape[0], slot)
    gm = cot_ref[...].astype(F32) + norm_back(dn_ref[...], mid_ref[...])
    gmid_ref[...] = gm
    ga = jnp.where(valid, gm, 0.0).astype(BF)
    gatt = sum(nt(ga[:, i * GW : (i + 1) * GW], w[...]) for i, w in enumerate(wo_refs))
    gatt_ref[...] = gatt.astype(BF)
    part = tn(jnp.concatenate([a[...] for a in att_refs], axis=1), ga)

    @pl.when(c == 0)
    def _():
        acc_ref[...] = part

    @pl.when(c != 0)
    def _():
        acc_ref[...] += part

    @pl.when(c == pl.num_programs(0) - 1)
    def _():
        dwo_ref[...] = acc_ref[...].astype(BF)


def mid_grad(ids, cot, mid, dn, atts, weights, slot, tile):
    n, d = cot.shape
    rows = lambda w: pl.BlockSpec((tile, w), lambda c, *_: (c, 0))
    wos, wo_specs = out_weights(weights, d)
    return pl.pallas_call(
        functools.partial(mid_grad_kernel, slot, len(atts)),
        grid_spec=pltpu.PrefetchScalarGridSpec(
            num_scalar_prefetch=1,
            grid=(n // tile,),
            in_specs=[rows(d)] * 3 + [rows(a.shape[1]) for a in atts] + wo_specs,
            out_specs=[rows(d), rows(d), pl.BlockSpec((d, d), lambda c, *_: (0, 0))],
            scratch_shapes=[pltpu.VMEM((d, d), F32)],
        ),
        out_shape=[
            jax.ShapeDtypeStruct((n, d), F32),
            jax.ShapeDtypeStruct((n, d), BF),
            jax.ShapeDtypeStruct((d, 3 * d), BF),
        ],
        compiler_params=params(),
        cost_estimate=cost(4 * n * d * d, 18 * n * d),
        name="mid_grad",
    )(ids, cot, mid, dn, *atts, *wos)


def input_grad_kernel(n_group, *refs):
    g_refs, w_refs = refs[:n_group], refs[n_group : 4 * n_group]
    x_ref, gmid_ref = refs[4 * n_group : 4 * n_group + 2]
    out_ref = refs[-1]
    e = 0.0
    for i, g in enumerate(g_refs):
        w = jnp.concatenate([w[...] for w in w_refs[3 * i : 3 * i + 3]], axis=1)
        e = e + nt(g[...], w)
    out_ref[...] = gmid_ref[...] + norm_back(e, x_ref[...].astype(F32))


def input_grad(gqkvs, weights, x, gmid, rows, start, stop, filled=None):
    n, d = x.shape
    arrays = [(w, 4 * g + i) for w in weights for g in range(w.shape[1] // (4 * GW)) for i in range(3)]
    spec = lambda w: pl.BlockSpec((rows, w), lambda i: (start + i, 0))
    more = [] if filled is None else [filled]
    n_in = 4 * len(gqkvs) + 2
    count = (stop - start) * rows
    return pl.pallas_call(
        functools.partial(input_grad_kernel, len(gqkvs)),
        grid=(stop - start,),
        in_specs=[spec(3 * GW)] * len(gqkvs)
        + [pl.BlockSpec((d, GW), lambda i, g=g: (0, g)) for _, g in arrays]
        + [spec(d), spec(d)]
        + [pl.BlockSpec(memory_space=pl.ANY)] * len(more),
        out_specs=spec(d),
        out_shape=jax.ShapeDtypeStruct((n, d), F32),
        input_output_aliases={n_in: 0} if more else {},
        compiler_params=params(),
        cost_estimate=cost(6 * count * d * d, 16 * count * d),
        name="input_grad",
    )(*gqkvs, *[w for w, _ in arrays], x, gmid, *more)


def angle_tables(positions):
    frequency = 1.0 / 10000.0 ** (jnp.arange(HEAD_DIM // 4, dtype=F32) * 4.0 / HEAD_DIM)
    frequency = jnp.tile(frequency, 8)
    first = (jnp.arange(HALF) // (HEAD_DIM // 4)) % 2 == 0
    crops, _, slot = positions.shape
    place = jnp.where(first, positions[:, 0, :, None], positions[:, 1, :, None])
    angles = (place.astype(F32) * frequency).reshape(crops * slot, HALF)
    return jnp.cos(angles), jnp.sin(angles)


def rot_order(w):
    rows, cols = w.shape
    w = w.reshape(rows, cols // GW, GROUP, 2, HEAD_DIM // 2)
    return w.transpose(0, 1, 3, 2, 4).reshape(rows, cols)


def natural_order(w):
    rows, cols = w.shape
    w = w.reshape(rows, cols // GW, 2, GROUP, HEAD_DIM // 2)
    return w.transpose(0, 1, 3, 2, 4).reshape(rows, cols)


def join_attn(wq, wk, wv, wo, gain):
    scaled = [(w.astype(F32) * gain).astype(BF) for w in (rot_order(wq), rot_order(wk), wv)]
    return jnp.stack(scaled + [wo])


def swap(x, axis, bit, size):
    return lax.ppermute(x, axis, [(i, i ^ bit) for i in range(size)])


def shift(x, step, size):
    half = size // 2
    return lax.ppermute(x, "fsdp", [(((i // 2 + step) % half) * 2 + i % 2, i) for i in range(size)])


def pick(x, index, axis=0):
    return lax.dynamic_index_in_dim(x, index, axis, keepdims=False)


def total(*parts):
    return sum(p.astype(F32) for p in parts).astype(BF)


def along_z(mine, size):
    return jnp.stack([mine] + [shift(mine, k, size) for k in range(1, size // 2)])


def over_reps(x, reps):
    return jnp.stack([x] + [swap(x, "rep", bit, reps) for bit in range(1, reps)])


def sum_reps(x, reps):
    if reps != 4:
        return lax.psum(x, "rep").astype(F32)
    x = (x.astype(F32) + swap(x, "rep", 1, reps).astype(F32)).astype(BF)
    return x.astype(F32) + swap(x, "rep", 2, reps).astype(F32)


def body(tokens, cotangent, crop_heights, rope_positions, gain_attn, w_query, w_key, w_value, w_out,
         gain_mlp, w_gate, w_up, w_down, *, reps, size):
    crops = crop_heights.shape[0]
    n, d = tokens.shape
    slot = n // crops
    tile = TILE if n % TILE == 0 else slot
    gain1 = gain_attn.astype(F32)[:, None]
    gain2 = gain_mlp.astype(F32)[:, None]

    def gather(w):
        return lax.all_gather(w, "fsdp", axis=0, tiled=True)

    def scatter(g):
        return lax.psum_scatter(g, "fsdp", scatter_dimension=0, tiled=True)

    def reduce(g):
        return sum_reps(scatter(g), reps)

    pin = lax.optimization_barrier
    links = reps == 4 and size == SHARDS
    rep, f = lax.axis_index("rep"), lax.axis_index("fsdp")
    joined = join_attn(w_query, w_key, w_value, w_out, gain1)
    if links:
        place = jnp.stack([rep, f // 2, f % 2]).astype(jnp.int32)
        mine = pick(joined, rep)
        mine, w_gate, w_up, w_down, rope_positions = pin((mine, w_gate, w_up, w_down, rope_positions))
        lines = [along_z(m, size) for m in (mine[:, :GW], mine[:, GW:])]
        lines[0], tokens_1 = pin((lines[0], tokens))
        sides = [swap(lines[0], "rep", bit, reps) for bit in range(1, reps)]
    else:
        place = jnp.zeros((3,), jnp.int32)
        every = lax.all_gather(joined, "fsdp", axis=1, tiled=True)
        every = every.reshape(4, SHARDS // 2, 2, d // SHARDS, d)
    ids = jnp.concatenate([crop_heights, place])
    cos, sin = angle_tables(rope_positions)
    if not links:
        tokens_1 = tokens
    nm1 = norm_call(tokens_1, tile)
    if links:
        *sides, lines[1], nm1, cos, sin = pin((*sides, lines[1], nm1, cos, sin))
        own = jnp.stack([lines[0]] + sides)
        own, w_gate, w_up, w_down = pin((own, w_gate, w_up, w_down))
        oth = swap(own, "fsdp", 1, size)
    scaled = [(w.astype(F32) * gain2).astype(BF) for w in (w_gate, w_up)]
    split = list(zip(halves(scaled[0], 1), halves(scaled[1], 1), halves(w_down, 0)))
    if size == SHARDS:
        packs = [lax.all_gather(pack_mlp(*part), "fsdp", axis=0, tiled=False) for part in split]
    else:
        wide = [gather(w).reshape(SHARDS, -1, w.shape[1]) for w in scaled]
        down = gather(w_down).reshape(SHARDS, -1, d)
        split = zip(*[[jnp.stack(h) for h in zip(*[halves(w, a) for w in ws])] for ws, a in
                      ((wide[0], 1), (wide[1], 1), (down, 0))])
        packs = [jax.vmap(pack_mlp)(*part) for part in split]

    attended, weights = [], []
    for i, cols in enumerate((slice(0, GW), slice(GW, d))):
        if not links:
            own, oth = every[:, :, 0, :, cols], every[:, :, 1, :, cols]
        elif i:
            *parts, _ = pin((lines[1], *sides, atts))
            own = jnp.stack(parts)
            oth = swap(own, "fsdp", 1, size)
        else:
            sides = [swap(lines[1], "rep", bit, reps) for bit in range(1, reps)]
        *some, w = attn_fwd(ids, nm1, cos, sin, own, oth, slot)
        attended.append(some)
        weights.append(w)
        atts = [a for _, a, _ in attended]
    mid, nm2 = out_proj(ids, tokens, atts, weights, slot, tile)
    part, dn, grad_a = mlp(ids, nm2, cotangent, mid, None, packs[0], slot, tile)
    out, dn, grad_b = mlp(ids, nm2, cotangent, part, dn, packs[1], slot, tile)
    local_a = scatter(grad_a.reshape(-1, PACK)) if size == SHARDS else grad_a
    local_b = scatter(grad_b.reshape(-1, PACK)) if size == SHARDS else grad_b
    gmid, gatt, joint = mid_grad(ids, cotangent, mid, dn, atts, weights, slot, tile)

    def backward(index, gatt, joint=None):
        w = 0 if index == 0 else 1
        qkv, att, lse = attended[w]
        return attn_bwd(qkv, gatt, att, lse, nm1, cos, sin, slot, index - w, w, joint)

    fast = size == SHARDS
    if links:
        local_a, gatt = pin((local_a, gatt))
        local_a = total(local_a, swap(local_a, "rep", 1, reps))
    gqkv0, joint = backward(0, gatt, joint)
    if links:
        local_a, gatt, gqkv0 = pin((local_a, gatt, gqkv0))
        other_a = swap(local_a, "rep", 2, reps)
    gqkv1, joint = backward(1, gatt, joint)
    if links:
        other_a, local_b, joint, gatt, gqkv1 = pin((other_a, local_b, joint, gatt, gqkv1))
        local_b = total(local_b, swap(local_b, "rep", 1, reps))
    joint = scatter(joint)
    gqkv2, dw2 = backward(2, gatt)
    gqkvs = [gqkv0, gqkv1, gqkv2]
    part = tile // 3 if tile % 48 == 0 else tile
    count = n // part
    cuts = [0, count // 3, 2 * count // 3, count]
    grad = lambda i, gmid, filled: input_grad(
        gqkvs, weights, tokens, gmid, part, cuts[i], cuts[i + 1], filled
    )
    if links:
        y, x, z, core = rep // 2, rep % 2, f // 2, f % 2
        zs, rows = size // 2, d // size
        cut = dw2.reshape(zs, 2, 2, 2, rows // reps, 3 * GW)
        keep, send = pick(cut, core, 1), pick(cut, 1 - core, 1)
        got = swap(send, "fsdp", 1, size)
        keep, local_b, gqkvs[2] = pin((keep, local_b, gqkvs[2]))
        other_b = swap(local_b, "rep", 2, reps)
        grad_tokens = grad(0, gmid, None)
        grad_tokens, keep, got, joint, other_b = pin((grad_tokens, keep, got, joint, other_b))
        side = swap(total(pick(keep, 1 - x, 2), pick(got, 1 - x, 2)), "rep", 1, reps)
        joint_x = swap(joint, "rep", 1, reps)
        keep = total(pick(keep, x, 2), pick(got, x, 2))
        keep, gmid = pin((keep, gmid))
        grad_tokens = grad(1, gmid, grad_tokens)
        grad_tokens, keep, side, joint_x = pin((grad_tokens, keep, side, joint_x))
        got = swap(total(pick(keep, 1 - y, 1), pick(side, 1 - y, 1)), "rep", 2, reps)
        joint = total(joint, joint_x)
        joint_y = swap(joint, "rep", 2, reps)
        keep, side = pick(keep, y, 1), pick(side, y, 1)
        keep, side, gmid = pin((keep, side, gmid))
        grad_tokens = grad(2, gmid, grad_tokens)
        grad_tokens, keep, side, got, joint_y = pin((grad_tokens, keep, side, got, joint_y))

        def at(k):
            i = (z + k) % zs
            return total(pick(keep, i), pick(side, i), pick(got, i))

        part = total(at(0), *[shift(at(zs - k), k, size) for k in range(1, zs)])
        every = over_reps(part, reps)
        dw2 = jnp.concatenate([pick(every, r ^ rep) for r in range(reps)], axis=0).astype(F32)
        joint = joint.astype(F32) + joint_y.astype(F32)
        sum_a = local_a.astype(F32) + other_a.astype(F32)
        sum_b = local_b.astype(F32) + other_b.astype(F32)
    else:
        grad_tokens = None
        for i in range(3):
            grad_tokens = grad(i, gmid, grad_tokens)
        dw2 = reduce(dw2)
        joint = sum_reps(joint, reps)
        if fast:
            sum_a, sum_b = sum_reps(local_a, reps), sum_reps(local_b, reps)
    dwo, dws = joint[:, :d], [joint[:, d : d + 3 * GW], joint[:, d + 3 * GW :], dw2]

    both = []
    if fast:
        both = [unpack_mlp(x, d // SHARDS, d) for x in (sum_a, sum_b)]
    else:
        both = [jax.vmap(lambda p: unpack_mlp(p, d // SHARDS, d))(grad) for grad in (grad_a, grad_b)]

    def rejoin(pair, axis):
        lead = pair[0].shape[:axis]
        rest = pair[0].shape[axis + 1 :]
        parts = [p.reshape(lead + (SHARDS if axis else 1, -1) + rest) for p in pair]
        return jnp.stack(parts, axis=axis + 1).reshape(lead + (-1,) + rest)

    if size == SHARDS:
        raw = [rejoin([b[i] for b in both], axis) for i, axis in ((0, 1), (1, 1), (2, 0))]
    else:
        raw = []
        for i, axis in ((0, 1), (1, 1), (2, 0)):
            whole = jax.vmap(lambda a, b: rejoin([a, b], axis))(both[0][i], both[1][i])
            raw.append(reduce(whole.reshape(-1, whole.shape[-1])))
    g2 = jnp.sum(raw[0] * w_gate.astype(F32), axis=1) + jnp.sum(raw[1] * w_up.astype(F32), axis=1)
    dwg, dwu, dwd = raw[0] * gain2, raw[1] * gain2, raw[2]

    raw = [jnp.concatenate([w[:, i * GW : (i + 1) * GW] for w in dws], axis=1) for i in range(3)]
    raw = [natural_order(raw[0]), natural_order(raw[1]), raw[2]]
    g1 = sum(jnp.sum(r * w.astype(F32), axis=1) for r, w in zip(raw, (w_query, w_key, w_value)))
    dwq, dwk, dwv = (r * gain1 for r in raw)
    return out, grad_tokens, g1, dwq, dwk, dwv, dwo, g2, dwg, dwu, dwd


def solution(mesh):
    in_specs = (
        P(("rep", "fsdp"), None),
        P(("rep", "fsdp"), None),
        P(("rep", "fsdp")),
        P(("rep", "fsdp"), None, None),
        P("fsdp"),
        P("fsdp", None),
        P("fsdp", None),
        P("fsdp", None),
        P("fsdp", None),
        P("fsdp"),
        P("fsdp", None),
        P("fsdp", None),
        P("fsdp", None),
    )
    out_specs = (
        P(("rep", "fsdp"), None),
        P(("rep", "fsdp"), None),
        P("fsdp"),
        P("fsdp", None),
        P("fsdp", None),
        P("fsdp", None),
        P("fsdp", None),
        P("fsdp"),
        P("fsdp", None),
        P("fsdp", None),
        P("fsdp", None),
    )
    sizes = dict(reps=mesh.shape["rep"], size=mesh.shape["fsdp"])
    return jax.shard_map(functools.partial(body, **sizes), mesh=mesh, in_specs=in_specs, out_specs=out_specs, check_vma=False)
```

time: 605 us -> 404 us (0.67); the launches traced: 605 us -> 397 us
  waiting for transfers between devices: 264 us -> 23.8 us
  starting transfers between devices: 0.43 us -> 36.9 us
  blocking collectives: 13.5 us -> 0 us
  other arithmetic: 15.7 us -> 25.8 us
  Pallas kernels: 286 us -> 276 us
  local copies, waits for them, and re-layouts: 11.1 us -> 18.9 us
    reduce_scatter x5 -> x3, waiting for transfers between devices: 119 us -> 0.04 us  [scatter(): return lax.psum_scatter(g, 'fsdp', scatter_dimension=0, tiled=True)]
    all_gather x5 -> x2, waiting for transfers between devices: 89.5 us -> 0.02 us  [body(): lax.all_gather(pack_mlp(*part), 'fsdp', axis=0, tiled=False)]
    psum x1 -> x0, waiting for transfers between devices: 50.8 us -> none  [reduce(): return lax.psum(local, 'rep').astype(F32)]
    ppermute x0 -> x29, starting transfers between devices: none -> 36.5 us  [the longest x20 19.3 us: swap(): return lax.ppermute(x, axis, [(i, i ^ bit) for i in range(size)])]
    ppermute x0 -> x29, waiting for transfers between devices: none -> 23.6 us  [the longest x20 17.1 us: swap(): return lax.ppermute(x, axis, [(i, i ^ bit) for i in range(size)])]
    all_gather x1 -> x0, blocking collectives: 13.5 us -> none  [body(): lax.all_gather(jnp.stack([gain_attn, gain_mlp]), 'fsdp', axis=1, tiled=True)]
    pallas_call x7 -> x13, Pallas kernels: 286 us -> 276 us  [the longest x2 92.6 us: mlp(): pl.pallas_call(functools.partial(mlp_kernel, slot, final, step), grid_spe...]
  transfers between devices with their start and end apart: 11 -> 34, of which waited for: 7 -> 10; matrix products, arithmetic and copies ran while one was open for 2% -> 5% of each run, Pallas kernels for 27% -> 70%
where the time goes in v2:
time: 404 us; the launch traced here: 397 us
  Pallas kernels  276 us (68%)
  starting transfers between devices  36.9 us (9%)
  other arithmetic  25.8 us (6%)
  waiting for transfers between devices  23.8 us (6%)
  local copies, waits for them, and re-layouts  18.9 us (5%)
  between operations  15.5 us (4%)
    pallas_call x2, Pallas kernels, mlp(): pl.pallas_call(functools.partial(mlp_kernel, slot, final, step), grid_spe...  92.6 us
    pallas_call x3, Pallas kernels, attn_bwd(): pl.pallas_call(functools.partial(attn_bwd_kernel, slot, size), grid=(1, c...  74.9 us
    pallas_call x2, Pallas kernels, attn_fwd(): pl.pallas_call(functools.partial(attn_fwd_kernel, slot, size), grid_spec=...  48.9 us
    pallas_call x3, Pallas kernels, input_grad(): pl.pallas_call(functools.partial(input_grad_kernel, len(gqkvs)), grid=(st...  25.3 us
    ppermute x20, starting transfers between devices, swap(): return lax.ppermute(x, axis, [(i, i ^ bit) for i in range(size)])  19.3 us
    pallas_call x1, Pallas kernels, mid_grad(): pl.pallas_call(functools.partial(mid_grad_kernel, slot, len(atts)), grid_...  18.5 us
    ppermute x9, starting transfers between devices, shift(): lax.ppermute(x, 'fsdp', [((i // 2 + step) % half * 2 + i % 2, i) for i in...  17.2 us
    ppermute x20, waiting for transfers between devices, swap(): return lax.ppermute(x, axis, [(i, i ^ bit) for i in range(size)])  17.1 us
  transfers between devices with their start and end apart: 34, of which 10 were waited for; matrix products, arithmetic and copies ran while one was open for 5% of the time, Pallas kernels for 70%

profile of v2, /device:TPU:0, one launch (start us, length us, event | category | flops | bytes accessed | tf_op | source)
XLA Modules:
  0.0 396.8 jit_solution(16640433796245108253)
XLA Ops:
  7.9 1.1 copy.36
  10.6 5.1 %collective-permute-start = (bf16[96,256]{1,0:T(8,128)(2,1)S(1)}, bf16[96,256]{1,0:T(8,128)(2,1)S(1)}, u32[]{:S(2)}, u32[]{:S(2)}) collective-permute-start(bf16[96,256]{1,0:T(8,128)(2,1)S(1)} %get-tuple-element.220), channel_id=1, source_target_pairs={{2,0},{3,1},{4,2},{5,3},{6,4},{7,5},{0,6},{1,7},{10,8},{11,9},{12,... | collective-permute-start | bytes 147464 | tf_op jit(solution)/shard_map/ppermute | solution.py:646
  16.7 2.9 collective-permute-start.6
  19.6 1.1 collective-permute-start.7
  21.2 1.1 collective-permute-done.2
  22.3 1.6 collective-permute-start.3
  23.9 1.5 collective-permute-start.4
  25.9 9.1 %fusion = (f32[2304,128]{1,0:T(8,128)}, f32[2304,128]{1,0:T(8,128)}) fusion(f32[128]{0:T(128)S(1)} %mul.113, s32[2304]{0:T(1024)S(1)} %broadcast_in_dim.29, s32[2304]{0:T(1024)S(1)} %broadcast_in_dim.27, pred[128]{0:T(512)(128)(4,1)S(1)} %fusion.25), kind=kLoop, calls=%fused_computation.6 | loop fusion | flops 884736 | bytes 2378368 | tf_op jit(solution)/shard_map/sin | solution.py:620
  35.0 5.2 %norm_in.1.nm_ref = bf16[2304,768]{1,0:T(8,128)(2,1)} custom-call(bf16[2304,768]{1,0:T(8,128)(2,1)} %refs_12_.5), custom_call_target="tpu_custom_call" | custom-call | bytes 7077888 | tf_op jit(solution)/shard_map/norm_in/pallas_call | solution.py:52
  41.8 2.1 slice_reduce_fusion.1
  44.1 2.1 slice_reduce_fusion
  48.3 1.5 collective-permute-start.10
  49.8 1.5 collective-permute-start.11
  51.8 17.1 %attn_fwd.2 = (bf16[2304,768]{1,0:T(8,128)(2,1)}, bf16[2304,256]{1,0:T(8,128)(2,1)}, f32[1,4,8,576]{3,2,1,0:T(8,128)}, bf16[4,2,96,1024]{3,2,1,0:T(8,128)(2,1)}) custom-call(s32[7]{0:T(128)} %pad_add_fusion.ids_ref, bf16[2304,768]{1,0:T(8,128)(2,1)} %norm_in.1.nm_ref, f32[2304,128]{1,0:T(8,128)} %get-tuple-element.95.cos_ref, ...), custom_call_target="tpu_custom_call" | custom-call | flops 18432000000 | bytes 3538944 | tf_op jit(solution)/shard_map/attn_fwd/pallas_call | solution.py:162
  69.9 1.0 copy-done.14
  71.0 2.2 collective-permute-done.13.oth_hbm
  73.3 31.8 %attn_fwd.3 = (bf16[2304,1536]{1,0:T(8,128)(2,1)}, bf16[2304,512]{1,0:T(8,128)(2,1)}, f32[2,4,8,576]{3,2,1,0:T(8,128)}, bf16[4,2,96,2048]{3,2,1,0:T(8,128)(2,1)}) custom-call(s32[7]{0:T(128)} %pad_add_fusion.ids_ref, bf16[2304,768]{1,0:T(8,128)(2,1)} %norm_in.1.nm_ref, f32[2304,128]{1,0:T(8,128)} %get-tuple-element.95.cos_ref, ...), custom_call_target="tpu_custom_call" | custom-call | flops 36864000000 | bytes 3538944 | tf_op jit(solution)/shard_map/attn_fwd/pallas_call | solution.py:162
  105.1 10.7 %out_proj.1 = (f32[2304,768]{1,0:T(8,128)}, bf16[2304,768]{1,0:T(8,128)(2,1)}) custom-call(s32[7]{0:T(128)} %pad_add_fusion.ids_ref, bf16[2304,768]{1,0:T(8,128)(2,1)} %refs_12_.5, bf16[2304,256]{1,0:T(8,128)(2,1)} %get-tuple-element.104.refs_0_.att_ref, bf16[2304,512]{1,0:T(8,128)(2,1)} %get-tuple-element.110.refs_1_.att_ref, bf16[768,1024]{1,0:T(8,128)(2,1)} %bitcast.171, ...), custom_call_target="tpu_custom_call" | custom-call | flops 2717908992 | bytes 17694720 | tf_op jit(solution)/shard_map/out_proj/pallas_call | solution.py:344
  115.7 45.8 %mlp.2 = (f32[2304,768]{1,0:T(8,128)}, f32[2304,768]{1,0:T(8,128)}, bf16[8,576,512]{2,1,0:T(8,128)(2,1)}) custom-call(s32[7]{0:T(128)} %pad_add_fusion.ids_ref, bf16[2304,768]{1,0:T(8,128)(2,1)} %get-tuple-element.113.nm_ref, bf16[2304,768]{1,0:T(8,128)(2,1)} %cot_ref.5, f32[2304,768]{1,0:T(8,128)} %get-tuple-element.114.part_ref.mid_ref, ...), custom_call_target="tpu_custom_call" | custom-call | flops 55296000000 | bytes 35389440 | tf_op jit(solution)/shard_map/mlp/pallas_call | solution.py:501
  161.6 46.9 %mlp.3 = (bf16[2304,768]{1,0:T(8,128)(2,1)}, f32[2304,768]{1,0:T(8,128)}, bf16[8,576,512]{2,1,0:T(8,128)(2,1)}) custom-call(s32[7]{0:T(128)} %pad_add_fusion.ids_ref, bf16[2304,768]{1,0:T(8,128)(2,1)} %get-tuple-element.113.nm_ref, bf16[2304,768]{1,0:T(8,128)(2,1)} %cot_ref.5, f32[2304,768]{1,0:T(8,128)} %get-tuple-element.118.part_ref, ...), custom_call_target="tpu_custom_call" | custom-call | flops 55296000000 | bytes 35389440 | tf_op jit(solution)/shard_map/mlp/pallas_call | solution.py:501
  208.6 18.5 %mid_grad.1 = (f32[2304,768]{1,0:T(8,128)}, bf16[2304,768]{1,0:T(8,128)(2,1)}, bf16[768,2304]{1,0:T(8,128)(2,1)}) custom-call(s32[7]{0:T(128)} %pad_add_fusion.ids_ref, bf16[2304,768]{1,0:T(8,128)(2,1)} %cot_ref.5, f32[2304,768]{1,0:T(8,128)} %get-tuple-element.114.part_ref.mid_ref, f32[2304,768]{1,0:T(8,128)} %get-tuple-element.122.dn_ref, ...), custom_call_target="tpu_custom_call" | custom-call | flops 5435817984 | bytes 31850496 | tf_op jit(solution)/shard_map/mid_grad/pallas_call | solution.py:559
  227.1 1.4 collective-permute-start.14
  228.4 24.9 %attn_bwd.3 = (bf16[2304,768]{1,0:T(8,128)(2,1)}, bf16[768,2304]{1,0:T(8,128)(2,1)}) custom-call(bf16[2304,768]{1,0:T(8,128)(2,1)} %get-tuple-element.126.qkv_ref, bf16[2304,768]{1,0:T(8,128)(2,1)} %get-tuple-element.140.go_ref, bf16[2304,256]{1,0:T(8,128)(2,1)} %get-tuple-element.104.refs_0_.att_ref, ...), custom_call_target="tpu_custom_call", output_to_operand_aliasing={{1}: (7, {})} | custom-call | flops 27648000000 | bytes 3538944 | tf_op jit(solution)/shard_map/attn_bwd/pallas_call | solution.py:279
  253.6 1.4 collective-permute-start.15
  255.0 25.1 %attn_bwd.4 = (bf16[2304,768]{1,0:T(8,128)(2,1)}, bf16[768,2304]{1,0:T(8,128)(2,1)}) custom-call(bf16[2304,1536]{1,0:T(8,128)(2,1)} %get-tuple-element.133.qkv_ref, bf16[2304,768]{1,0:T(8,128)(2,1)} %get-tuple-element.140.go_ref, bf16[2304,512]{1,0:T(8,128)(2,1)} %get-tuple-element.110.refs_1_.att_ref, ...), custom_call_target="tpu_custom_call", output_to_operand_aliasing={{1}: (7, {})} | custom-call | flops 27648000000 | bytes 3538944 | tf_op jit(solution)/shard_map/attn_bwd/pallas_call | solution.py:279
  282.1 24.9 %attn_bwd.5 = (bf16[2304,768]{1,0:T(8,128)(2,1)}, bf16[768,768]{1,0:T(8,128)(2,1)}) custom-call(bf16[2304,1536]{1,0:T(8,128)(2,1)} %get-tuple-element.133.qkv_ref, bf16[2304,768]{1,0:T(8,128)(2,1)} %get-tuple-element.140.go_ref, bf16[2304,512]{1,0:T(8,128)(2,1)} %get-tuple-element.110.refs_1_.att_ref, f32[2,4,8,576]{3,2,1,0:T(8,128)} %get-tuple-element.135.lse_ref, ...), custom_call_target="tpu_custom_call" | custom-call | flops 27648000000 | bytes 3538944 | tf_op jit(solution)/shard_map/attn_bwd/pallas_call | solution.py:279
  307.1 1.5 copy-done.12
  309.7 1.2 add_convert_fusion
  311.7 8.7 %input_grad.3.refs_14_ = f32[2304,768]{1,0:T(8,128)} custom-call(bf16[2304,768]{1,0:T(8,128)(2,1)} %get-tuple-element.130.refs_0_, bf16[2304,768]{1,0:T(8,128)(2,1)} %get-tuple-element.139.refs_1_, bf16[2304,768]{1,0:T(8,128)(2,1)} %get-tuple-element.144.refs_2_, bf16[768,1024]{1,0:T(8,128)(2,1)} %bitcast.173, bf16[768,1024]{1,0:T(8,128)(2,1)} %bitcast.174, ...), custom_call_target="tpu_custom_call" | custom-call | flops 2717908992 | bytes 9437184 | tf_op jit(solution)/shard_map/input_grad/pallas_call | solution.py:597
  320.4 6.4 %collective-permute-done.18 = bf16[576,512]{1,0:T(8,128)(2,1)} collective-permute-done((bf16[576,512]{1,0:T(8,128)(2,1)S(1)}, bf16[576,512]{1,0:T(8,128)(2,1)}, u32[]{:S(2)}, u32[]{:S(2)}) %collective-permute-start.18) | collective-permute-done | bytes 589856 | tf_op jit(solution)/shard_map/ppermute | solution.py:641
  326.8 1.2 convert_add_fusion
  332.9 1.1 fusion.10
  334.0 1.2 collective-permute-start.19
  335.2 1.0 fusion.9
  337.3 1.5 broadcast_multiply_fusion
  340.3 8.3 %input_grad.4.refs_14_ = f32[2304,768]{1,0:T(8,128)} custom-call(bf16[2304,768]{1,0:T(8,128)(2,1)} %get-tuple-element.130.refs_0_, bf16[2304,768]{1,0:T(8,128)(2,1)} %get-tuple-element.139.refs_1_, bf16[2304,768]{1,0:T(8,128)(2,1)} %get-tuple-element.144.refs_2_, bf16[768,1024]{1,0:T(8,128)(2,1)} %bitcast.176, ...), custom_call_target="tpu_custom_call", output_to_operand_aliasing={{}: (14, {})} | custom-call | flops 2717908992 | bytes 9437184 | tf_op jit(solution)/shard_map/input_grad/pallas_call | solution.py:597
  348.6 3.6 collective-permute-done.20
  353.8 1.6 collective-permute-start.21
  356.3 8.3 %input_grad.5 = f32[2304,768]{1,0:T(8,128)} custom-call(bf16[2304,768]{1,0:T(8,128)(2,1)} %get-tuple-element.130.refs_0_, bf16[2304,768]{1,0:T(8,128)(2,1)} %get-tuple-element.139.refs_1_, bf16[2304,768]{1,0:T(8,128)(2,1)} %get-tuple-element.144.refs_2_, bf16[768,1024]{1,0:T(8,128)(2,1)} %bitcast.179, ...), custom_call_target="tpu_custom_call", output_to_operand_aliasing={{}: (14, {})} | custom-call | flops 2717908992 | bytes 9437184 | tf_op jit(solution)/shard_map/input_grad/pallas_call | solution.py:597
  364.7 1.8 collective-permute-done.21
  366.5 2.8 collective-permute-start.23
  369.2 4.1 %collective-permute-start.24 = (bf16[24,768]{1,0:T(8,128)(2,1)S(1)}, bf16[24,768]{1,0:T(8,128)(2,1)S(1)}, u32[]{:S(2)}, u32[]{:S(2)}) collective-permute-start(bf16[24,768]{1,0:T(8,128)(2,1)S(1)} %get-tuple-element.201), channel_id=1, source_target_pairs={{4,0},{5,1},{6,2},{7,3},{0,4},{1,5},{2,6},{3,7},{12,8},{13,9},{14,... | collective-permute-start | bytes 110600 | tf_op jit(solution)/shard_map/ppermute | solution.py:646
  373.8 2.6 collective-permute-done.24
  376.5 2.6 collective-permute-done.25
  379.5 1.6 collective-permute-start.27
  381.1 1.6 collective-permute-start.28
  383.5 2.5 collective-permute-done.28
  388.2 1.1 fusion.11
  (208 shorter events, 27.6 us)
Async XLA Ops:
  7.2 108.6 %all-gather.5.cloned.1.call-start = ((), (), s32[]{:S(2)}) async-start(), calls=%async_computation.6 | async-start | bytes 5308416 | tf_op jit(solution)/shard_map/all_gather | solution.py:718
  9.7 11.1 %copy-start.25 = (s32[4,2,576]{2,1,0:T(2,128)S(1)}, s32[4,2,576]{2,1,0:T(2,128)}, u32[]{:S(2)}) copy-start(s32[4,2,576]{2,1,0:T(2,128)} %param.16) | copy-start | bytes 55300
  10.6 24.4 %copy-start.31 = (bf16[96]{0:T(256)(128)(2,1)S(1)}, bf16[96]{0:T(256)(128)(2,1)}, u32[]{:S(2)}) copy-start(bf16[96]{0:T(256)(128)(2,1)} %param.22) | copy-start | bytes 580
  10.6 10.5 %collective-permute-start = (bf16[96,256]{1,0:T(8,128)(2,1)S(1)}, bf16[96,256]{1,0:T(8,128)(2,1)S(1)}, u32[]{:S(2)}, u32[]{:S(2)}) collective-permute-start(bf16[96,256]{1,0:T(8,128)(2,1)S(1)} %get-tuple-element.220), channel_id=1, source_target_pairs={{2,0},{3,1},{4,2},{5,3},{6,4},{7,5},{0,6},{1,7},{10,8},{11,9},{12,... | collective-permute-start | bytes 147464 | tf_op jit(solution)/shard_map/ppermute | solution.py:646
  15.7 5.4 %collective-permute-start.1 = (bf16[96,256]{1,0:T(8,128)(2,1)S(1)}, bf16[96,256]{1,0:T(8,128)(2,1)S(1)}, u32[]{:S(2)}, u32[]{:S(2)}) collective-permute-start(bf16[96,256]{1,0:T(8,128)(2,1)S(1)} %get-tuple-element.220), channel_id=1, source_target_pairs={{4,0},{5,1},{6,2},{7,3},{0,4},{1,5},{2,6},{3,7},{12,8},{13,9},{14,... | collective-permute-start | bytes 147464 | tf_op jit(solution)/shard_map/ppermute | solution.py:646
  15.7 6.6 %collective-permute-start.2 = (bf16[96,256]{1,0:T(8,128)(2,1)S(1)}, bf16[96,256]{1,0:T(8,128)(2,1)S(1)}, u32[]{:S(2)}, u32[]{:S(2)}) collective-permute-start(bf16[96,256]{1,0:T(8,128)(2,1)S(1)} %get-tuple-element.220), channel_id=1, source_target_pairs={{6,0},{7,1},{0,2},{1,3},{2,4},{3,5},{4,6},{5,7},{14,8},{15,9},{8,1... | collective-permute-start | bytes 147464 | tf_op jit(solution)/shard_map/ppermute | solution.py:646
  16.7 8.6 %collective-permute-start.6 = (bf16[96,512]{1,0:T(8,128)(2,1)S(1)}, bf16[96,512]{1,0:T(8,128)(2,1)S(1)}, u32[]{:S(2)}, u32[]{:S(2)}) collective-permute-start(bf16[96,512]{1,0:T(8,128)(2,1)S(1)} %get-tuple-element.218), channel_id=1, source_target_pairs={{2,0},{3,1},{4,2},{5,3},{6,4},{7,5},{0,6},{1,7},{10,8},{11,9},{12,... | collective-permute-start | bytes 294920 | tf_op jit(solution)/shard_map/ppermute | solution.py:646
  19.6 20.6 %collective-permute-start.7 = (bf16[96,512]{1,0:T(8,128)(2,1)S(1)}, bf16[96,512]{1,0:T(8,128)(2,1)S(1)}, u32[]{:S(2)}, u32[]{:S(2)}) collective-permute-start(bf16[96,512]{1,0:T(8,128)(2,1)S(1)} %get-tuple-element.218), channel_id=1, source_target_pairs={{4,0},{5,1},{6,2},{7,3},{0,4},{1,5},{2,6},{3,7},{12,8},{13,9},{14,... | collective-permute-start | bytes 294920 | tf_op jit(solution)/shard_map/ppermute | solution.py:646
  21.1 19.1 %collective-permute-start.8 = (bf16[96,512]{1,0:T(8,128)(2,1)S(1)}, bf16[96,512]{1,0:T(8,128)(2,1)S(1)}, u32[]{:S(2)}, u32[]{:S(2)}) collective-permute-start(bf16[96,512]{1,0:T(8,128)(2,1)S(1)} %get-tuple-element.218), channel_id=1, source_target_pairs={{6,0},{7,1},{0,2},{1,3},{2,4},{3,5},{4,6},{5,7},{14,8},{15,9},{8,1... | collective-permute-start | bytes 294920 | tf_op jit(solution)/shard_map/ppermute | solution.py:646
  22.3 17.9 %collective-permute-start.3 = (bf16[4,96,256]{2,1,0:T(8,128)(2,1)S(1)}, bf16[4,96,256]{2,1,0:T(8,128)(2,1)S(1)}, u32[]{:S(2)}, u32[]{:S(2)}) collective-permute-start(bf16[4,96,256]{2,1,0:T(8,128)(2,1)S(1)} %pad_maximum_fusion.9), channel_id=1, source_target_pairs={{0,8},{8,0},{16,24},{24,16},{1,9},{9,1},{17,25},{25,17},{2,10},{10... | collective-permute-start | bytes 589832 | tf_op jit(solution)/shard_map/ppermute | solution.py:641
  23.9 16.4 %collective-permute-start.4 = (bf16[4,96,256]{2,1,0:T(8,128)(2,1)S(1)}, bf16[4,96,256]{2,1,0:T(8,128)(2,1)S(1)}, u32[]{:S(2)}, u32[]{:S(2)}) collective-permute-start(bf16[4,96,256]{2,1,0:T(8,128)(2,1)S(1)} %pad_maximum_fusion.9), channel_id=1, source_target_pairs={{0,16},{8,24},{16,0},{24,8},{1,17},{9,25},{17,1},{25,9},{2,18},{10... | collective-permute-start | bytes 589832 | tf_op jit(solution)/shard_map/ppermute | solution.py:641
  25.4 14.9 %collective-permute-start.5 = (bf16[4,96,256]{2,1,0:T(8,128)(2,1)S(1)}, bf16[4,96,256]{2,1,0:T(8,128)(2,1)S(1)}, u32[]{:S(2)}, u32[]{:S(2)}) collective-permute-start(bf16[4,96,256]{2,1,0:T(8,128)(2,1)S(1)} %pad_maximum_fusion.9), channel_id=1, source_target_pairs={{0,24},{8,16},{16,8},{24,0},{1,25},{9,17},{17,9},{25,1},{2,26},{10... | collective-permute-start | bytes 589832 | tf_op jit(solution)/shard_map/ppermute | solution.py:641
  35.0 6.3 %copy-start.28 = (f32[96]{0:T(128)}, f32[96]{0:T(128)S(1)}, u32[]{:S(2)}) copy-start(f32[96]{0:T(128)S(1)} %convert_element_type.287) | copy-start | bytes 1156
  41.8 4.4 %copy-start.21 = (bf16[256,768]{1,0:T(8,128)(2,1)S(1)}, bf16[256,768]{1,0:T(8,128)(2,1)}, u32[]{:S(2)}) copy-start(bf16[256,768]{1,0:T(8,128)(2,1)} %param.25) | copy-start | bytes 1179652
  47.3 114.3 %all-gather.7.cloned.1.call-start = ((), (), s32[]{:S(2)}) async-start(), calls=%async_computation.7 | async-start | bytes 5308416 | tf_op jit(solution)/shard_map/all_gather | solution.py:718
  47.5 4.3 %collective-permute-start.9 = (bf16[4,4,96,256]{3,2,1,0:T(8,128)(2,1)S(1)}, bf16[4,4,96,256]{3,2,1,0:T(8,128)(2,1)}, u32[]{:S(2)}, u32[]{:S(2)}) collective-permute-start(bf16[4,4,96,256]{3,2,1,0:T(8,128)(2,1)S(1)} %copy-done.15), channel_id=1, source_target_pairs={{0,1},{1,0},{2,3},{3,2},{4,5},{5,4},{6,7},{7,6},{8,9},{9,8},{10,11... | collective-permute-start | bytes 2359304 | tf_op jit(solution)/shard_map/ppermute | solution.py:641
  48.3 20.6 %collective-permute-start.10 = (bf16[4,96,512]{2,1,0:T(8,128)(2,1)S(1)}, bf16[4,96,512]{2,1,0:T(8,128)(2,1)S(1)}, u32[]{:S(2)}, u32[]{:S(2)}) collective-permute-start(bf16[4,96,512]{2,1,0:T(8,128)(2,1)S(1)} %pad_maximum_fusion.5), channel_id=1, source_target_pairs={{0,8},{8,0},{16,24},{24,16},{1,9},{9,1},{17,25},{25,17},{2,10},{10... | collective-permute-start | bytes 1179656 | tf_op jit(solution)/shard_map/ppermute | solution.py:641
  49.8 19.6 %collective-permute-start.11 = (bf16[4,96,512]{2,1,0:T(8,128)(2,1)S(1)}, bf16[4,96,512]{2,1,0:T(8,128)(2,1)S(1)}, u32[]{:S(2)}, u32[]{:S(2)}) collective-permute-start(bf16[4,96,512]{2,1,0:T(8,128)(2,1)S(1)} %pad_maximum_fusion.5), channel_id=1, source_target_pairs={{0,16},{8,24},{16,0},{24,8},{1,17},{9,25},{17,1},{25,9},{2,18},{10... | collective-permute-start | bytes 1179656 | tf_op jit(solution)/shard_map/ppermute | solution.py:641
  51.3 18.1 %collective-permute-start.12 = (bf16[4,96,512]{2,1,0:T(8,128)(2,1)S(1)}, bf16[4,96,512]{2,1,0:T(8,128)(2,1)S(1)}, u32[]{:S(2)}, u32[]{:S(2)}) collective-permute-start(bf16[4,96,512]{2,1,0:T(8,128)(2,1)S(1)} %pad_maximum_fusion.5), channel_id=1, source_target_pairs={{0,24},{8,16},{16,8},{24,0},{1,25},{9,17},{17,9},{25,1},{2,26},{10... | collective-permute-start | bytes 1179656 | tf_op jit(solution)/shard_map/ppermute | solution.py:641
  69.6 3.6 copy-start.6
  69.6 3.6 collective-permute-start.13
  71.0 156.1 %reduce-scatter.4.cloned.1.call-start = ((), (), s32[]{:S(2)}) async-start(), calls=%async_computation.3 | async-start | bytes 5308416 | tf_op jit(solution)/shard_map/reduce_scatter | solution.py:685
  161.5 118.5 %reduce-scatter.6.cloned.1.call-start = ((), (), s32[]{:S(2)}) async-start(), calls=%async_computation.4 | async-start | bytes 5308416 | tf_op jit(solution)/shard_map/reduce_scatter | solution.py:685
  208.5 118.3 %reduce-scatter.8.cloned.1.call-start = ((), (), s32[]{:S(2)}) async-start(), calls=%async_computation.5 | async-start | bytes 3981312 | tf_op jit(solution)/shard_map/reduce_scatter | solution.py:685
  227.1 26.3 %collective-permute-start.14 = (bf16[576,512]{1,0:T(8,128)(2,1)}, bf16[576,512]{1,0:T(8,128)(2,1)S(1)}, u32[]{:S(2)}, u32[]{:S(2)}) collective-permute-start(bf16[576,512]{1,0:T(8,128)(2,1)} %reduce-scatter.4.cloned.1.call-done), channel_id=1, source_target_pairs={{0,8},{8,0},{16,24},{24,16},{1,9},{9,1},{17,25},{25,17},{2,10},{10... | collective-permute-start | bytes 1769480 | tf_op jit(solution)/shard_map/ppermute | solution.py:641
  228.4 24.9 %copy-start.19 = (bf16[576,512]{1,0:T(8,128)(2,1)S(1)}, bf16[576,512]{1,0:T(8,128)(2,1)}, u32[]{:S(2)}) copy-start(bf16[576,512]{1,0:T(8,128)(2,1)} %reduce-scatter.4.cloned.1.call-done) | copy-start | bytes 1769476
  253.6 26.5 %collective-permute-start.15 = (bf16[576,512]{1,0:T(8,128)(2,1)S(1)}, bf16[576,512]{1,0:T(8,128)(2,1)S(1)}, u32[]{:S(2)}, u32[]{:S(2)}) collective-permute-start(bf16[576,512]{1,0:T(8,128)(2,1)S(1)} %add_convert_fusion.1), channel_id=1, source_target_pairs={{0,16},{8,24},{16,0},{24,8},{1,17},{9,25},{17,1},{25,9},{2,18},{10... | collective-permute-start | bytes 1769480 | tf_op jit(solution)/shard_map/ppermute | solution.py:641
  281.1 28.5 %collective-permute-start.16 = (bf16[576,512]{1,0:T(8,128)(2,1)S(1)}, bf16[576,512]{1,0:T(8,128)(2,1)}, u32[]{:S(2)}, u32[]{:S(2)}) collective-permute-start(bf16[576,512]{1,0:T(8,128)(2,1)S(1)} %copy-done.18), channel_id=1, source_target_pairs={{0,8},{8,0},{16,24},{24,16},{1,9},{9,1},{17,25},{25,17},{2,10},{10... | collective-permute-start | bytes 1769480 | tf_op jit(solution)/shard_map/ppermute | solution.py:641
  307.1 4.5 %copy-start = (f32[576,512]{1,0:T(8,128)}, f32[576,512]{1,0:T(8,128)S(1)}, u32[]{:S(2)}) copy-start(f32[576,512]{1,0:T(8,128)S(1)} %convert_add_fusion.1) | copy-start | bytes 3538948
  309.6 10.8 %collective-permute-start.17 = (bf16[4,2,2,24,768]{4,3,1,0,2:T(8,128)(2,1)}, bf16[4,2,2,24,768]{4,3,1,0,2:T(8,128)(2,1)}, u32[]{:S(2)}, u32[]{:S(2)}) collective-permute-start(bf16[4,2,2,24,768]{4,3,1,0,2:T(8,128)(2,1)} %copy.48), channel_id=1, source_target_pairs={{0,1},{1,0},{2,3},{3,2},{4,5},{5,4},{6,7},{7,6},{8,9},{9,8},{10,11... | collective-permute-start | bytes 1769480 | tf_op jit(solution)/shard_map/ppermute | solution.py:641
  310.9 15.9 %collective-permute-start.18 = (bf16[576,512]{1,0:T(8,128)(2,1)S(1)}, bf16[576,512]{1,0:T(8,128)(2,1)}, u32[]{:S(2)}, u32[]{:S(2)}) collective-permute-start(bf16[576,512]{1,0:T(8,128)(2,1)S(1)} %add_convert_fusion), channel_id=1, source_target_pairs={{0,16},{8,24},{16,0},{24,8},{1,17},{9,25},{17,1},{25,9},{2,18},{10... | collective-permute-start | bytes 1769480 | tf_op jit(solution)/shard_map/ppermute | solution.py:641
  332.2 5.0 %copy-start.8 = (bf16[96,2048]{1,0:T(8,128)(2,1)S(1)}, bf16[96,2048]{1,0:T(8,128)(2,1)}, u32[]{:S(2)}) copy-start(bf16[96,2048]{1,0:T(8,128)(2,1)} %param.24) | copy-start | bytes 1179652
  332.2 5.0 %copy-start.29 = (f32[96]{0:T(128)S(1)}, f32[96]{0:T(128)}, u32[]{:S(2)}) copy-start(f32[96]{0:T(128)} %copy-done.28) | copy-start | bytes 1156
  332.9 3.3 copy-start.20
  332.9 4.4 %copy-start.10 = (bf16[96,2048]{1,0:T(8,128)(2,1)S(1)}, bf16[96,2048]{1,0:T(8,128)(2,1)}, u32[]{:S(2)}) copy-start(bf16[96,2048]{1,0:T(8,128)(2,1)} %param.23) | copy-start | bytes 1179652
  334.0 14.6 %collective-permute-start.19 = (bf16[4,2,24,768]{3,2,1,0:T(8,128)(2,1)S(1)}, bf16[4,2,24,768]{3,2,1,0:T(8,128)(2,1)}, u32[]{:S(2)}, u32[]{:S(2)}) collective-permute-start(bf16[4,2,24,768]{3,2,1,0:T(8,128)(2,1)S(1)} %fusion.10), channel_id=1, source_target_pairs={{0,8},{8,0},{16,24},{24,16},{1,9},{9,1},{17,25},{25,17},{2,10},{10... | collective-permute-start | bytes 884744 | tf_op jit(solution)/shard_map/ppermute | solution.py:641
  336.2 2.6 slice-start
  336.2 2.6 slice-start.1
  336.2 2.6 copy-start.22
  336.2 15.9 %collective-permute-start.20 = (bf16[96,2304]{1,0:T(8,128)(2,1)S(1)}, bf16[96,2304]{1,0:T(8,128)(2,1)S(1)}, u32[]{:S(2)}, u32[]{:S(2)}) collective-permute-start(bf16[96,2304]{1,0:T(8,128)(2,1)S(1)} %copy-done.20), channel_id=1, source_target_pairs={{0,8},{8,0},{16,24},{24,16},{1,9},{9,1},{17,25},{25,17},{2,10},{10... | collective-permute-start | bytes 1327112 | tf_op jit(solution)/shard_map/ppermute | solution.py:641
  352.3 14.1 %collective-permute-start.22 = (bf16[96,2304]{1,0:T(8,128)(2,1)S(1)}, bf16[96,2304]{1,0:T(8,128)(2,1)S(1)}, u32[]{:S(2)}, u32[]{:S(2)}) collective-permute-start(bf16[96,2304]{1,0:T(8,128)(2,1)S(1)} %add_convert_fusion.2), channel_id=1, source_target_pairs={{0,16},{8,24},{16,0},{24,8},{1,17},{9,25},{17,1},{25,9},{2,18},{10... | collective-permute-start | bytes 1327112 | tf_op jit(solution)/shard_map/ppermute | solution.py:641
  353.8 12.6 %collective-permute-start.21 = (bf16[4,24,768]{2,1,0:T(8,128)(2,1)S(1)}, bf16[4,24,768]{2,1,0:T(8,128)(2,1)S(1)}, u32[]{:S(2)}, u32[]{:S(2)}) collective-permute-start(bf16[4,24,768]{2,1,0:T(8,128)(2,1)S(1)} %fusion.12), channel_id=1, source_target_pairs={{0,16},{8,24},{16,0},{24,8},{1,17},{9,25},{17,1},{25,9},{2,18},{10... | collective-permute-start | bytes 442376 | tf_op jit(solution)/shard_map/ppermute | solution.py:641
  366.5 7.3 %collective-permute-start.23 = (bf16[24,768]{1,0:T(8,128)(2,1)S(1)}, bf16[24,768]{1,0:T(8,128)(2,1)S(1)}, u32[]{:S(2)}, u32[]{:S(2)}) collective-permute-start(bf16[24,768]{1,0:T(8,128)(2,1)S(1)} %get-tuple-element.199), channel_id=1, source_target_pairs={{2,0},{3,1},{4,2},{5,3},{6,4},{7,5},{0,6},{1,7},{10,8},{11,9},{12,... | collective-permute-start | bytes 110600 | tf_op jit(solution)/shard_map/ppermute | solution.py:646
  369.2 7.2 %collective-permute-start.24 = (bf16[24,768]{1,0:T(8,128)(2,1)S(1)}, bf16[24,768]{1,0:T(8,128)(2,1)S(1)}, u32[]{:S(2)}, u32[]{:S(2)}) collective-permute-start(bf16[24,768]{1,0:T(8,128)(2,1)S(1)} %get-tuple-element.201), channel_id=1, source_target_pairs={{4,0},{5,1},{6,2},{7,3},{0,4},{1,5},{2,6},{3,7},{12,8},{13,9},{14,... | collective-permute-start | bytes 110600 | tf_op jit(solution)/shard_map/ppermute | solution.py:646
  373.3 5.8 %collective-permute-start.25 = (bf16[24,768]{1,0:T(8,128)(2,1)S(1)}, bf16[24,768]{1,0:T(8,128)(2,1)S(1)}, u32[]{:S(2)}, u32[]{:S(2)}) collective-permute-start(bf16[24,768]{1,0:T(8,128)(2,1)S(1)} %get-tuple-element.200), channel_id=1, source_target_pairs={{6,0},{7,1},{0,2},{1,3},{2,4},{3,5},{4,6},{5,7},{14,8},{15,9},{8,1... | collective-permute-start | bytes 110600 | tf_op jit(solution)/shard_map/ppermute | solution.py:646
  379.1 4.4 %collective-permute-start.26 = (bf16[24,768]{1,0:T(8,128)(2,1)S(1)}, bf16[24,768]{1,0:T(8,128)(2,1)S(1)}, u32[]{:S(2)}, u32[]{:S(2)}) collective-permute-start(bf16[24,768]{1,0:T(8,128)(2,1)S(1)} %fusion.20), channel_id=1, source_target_pairs={{0,8},{8,0},{16,24},{24,16},{1,9},{9,1},{17,25},{25,17},{2,10},{10... | collective-permute-start | bytes 110600 | tf_op jit(solution)/shard_map/ppermute | solution.py:641
  379.5 4.0 collective-permute-start.27
  381.1 4.9 %collective-permute-start.28 = (bf16[24,768]{1,0:T(8,128)(2,1)S(1)}, bf16[24,768]{1,0:T(8,128)(2,1)S(1)}, u32[]{:S(2)}, u32[]{:S(2)}) collective-permute-start(bf16[24,768]{1,0:T(8,128)(2,1)S(1)} %fusion.20), channel_id=1, source_target_pairs={{0,24},{8,16},{16,8},{24,0},{1,25},{9,17},{17,9},{25,1},{2,26},{10... | collective-permute-start | bytes 110600 | tf_op jit(solution)/shard_map/ppermute | solution.py:641
  (20 other events, 23.5 us)
Sparse Core Ops, SparseCore 0:
  47.4 53.7 all-gather.4
  103.5 50.5 all-gather.6
  161.7 56.7 reduce-scatter.3
  220.6 53.3 reduce-scatter.5
  280.2 46.1 reduce-scatter.7
